TPU v7x, 32 devices: a whole 2x2x4 slice. The times are simulated.
32 devices in a mesh: groups: 2 (over y), rows: 4 (over z), cols: 4 (over x, core).
Axes of the slice: x: 2, y: 2, z: 4, core: 2. Of those that a mesh axis runs over, the one named last changes fastest.
Arguments:
- hidden: bfloat16 [64, 32, 1280], P(('groups', 'rows'), 'cols'), parts along dimension 0, may hold values from -6 to 6
- ln_gain: float32 [1280], replicated, may hold values from 0.1 to 1.9
- ln_bias: float32 [1280], replicated, may hold values from -3 to 3
- w_query: bfloat16 [1280, 256], P(None, 'cols'), may hold values from -8.944272 to 8.944272
- w_keyval: bfloat16 [1280, 512], P(None, 'cols'), may hold values from -0.3125 to 0.3125
- stale_keyval: bfloat16 [64, 32, 4, 128], P(('groups', 'rows'), None, 'cols'), parts along dimension 0, may hold values from -10 to 10
- w_out: bfloat16 [256, 1280], replicated, may hold values from -0.375 to 0.375
- out_bias: float32 [1280], replicated, may hold values from -3 to 3
Outputs:
- output_rows: bfloat16 [64, 32, 1280], P(('groups', 'rows'), 'cols'), parts along dimension 0
- fresh_keyval: bfloat16 [64, 32, 4, 128], P(('groups', 'rows'), None, 'cols'), parts along dimension 0
There are 2 independent parts, one for each index of `groups`. A program takes and returns all parts, laid end to end along the dimension named above; an argument that names none is the same for every part. Nothing has to cross between parts.
All inputs are finite; a program needn't handle non-finite values.
Results may differ from a plain program's by a relative error of at most 0.04.
The roundings to bfloat16 on the way count: a program that leaves them out, or rounds other values in their place, can miss the bound.
Values may be sent and summed in bfloat16 or wider, within the bound.
No kernel may reach another device: no remote copies, remote signals or barrier semaphores. Data moves between devices by JAX's collectives and lax.ppermute only.
A program may use at most 64 MiB of HBM per device.

v0:
```python
import functools
import math

import jax
import jax.numpy as jnp
from jax import lax
from jax.experimental import pallas as pl
from jax.experimental.pallas import tpu as pltpu
from jax.sharding import PartitionSpec as P


SCORE_BUDGET = 1 << 17
VMEM = pl.BlockSpec(memory_space=pltpu.VMEM)
PARAMS = pltpu.CompilerParams(vmem_limit_bytes=24 << 20)
HBM = pl.BlockSpec(memory_space=pltpu.HBM)
SMEM = pl.BlockSpec(memory_space=pltpu.SMEM)


def near(*arrays):
    return [pltpu.with_memory_space_constraint(a, pltpu.VMEM) for a in arrays]


def swap(block, axis, mask):
    size = lax.axis_size(axis)
    return lax.ppermute(block, axis, [(i, i ^ mask) for i in range(size)])


def gather_plan(size):
    plan = []
    for mask in range(1, size):
        low = mask & -mask
        plan.append((mask, mask - low, low))
    return sorted(plan, key=lambda step: (bin(step[0]).count("1"), -step[2]))


def gather_bands(block, axis):
    return [block] + [swap(block, axis, m) for m in range(1, lax.axis_size(axis))]


def gather_by_mask(block, axis):
    size = lax.axis_size(axis)
    blocks = {0: block}
    for mask, source, bit in gather_plan(size):
        blocks[mask] = swap(blocks[source], axis, bit)
    return [blocks[m] for m in range(size)]


def project_rows(strips, gain, bias, w_query, w_keyval, q_out, kv_out):
    scale, shift = gain[...].reshape(1, -1), bias[...].reshape(1, -1)
    normed = []
    for strip in strips:
        values = strip[...].astype(jnp.float32)
        centred = values - jnp.mean(values, axis=-1, keepdims=True)
        variance = jnp.mean(centred * centred, axis=-1, keepdims=True)
        normed.append(
            (centred * lax.rsqrt(variance + 1e-05) * scale + shift).astype(jnp.bfloat16)
        )
    both = jnp.concatenate(normed, axis=0)
    queries = lax.dot_general(
        both, w_query[...], (((1,), (1,)), ((), ())), preferred_element_type=jnp.float32
    ).astype(jnp.bfloat16)
    q_out[...] = jnp.concatenate([queries, jnp.zeros_like(queries)], axis=1)
    kv_out[...] = jnp.dot(both, w_keyval[...], preferred_element_type=jnp.float32).astype(
        jnp.bfloat16
    )


def load_kernel(count, *refs):
    sources, targets, arrived = refs[:count], refs[count:-1], refs[-1]
    copies = [
        pltpu.make_async_copy(source, target, arrived.at[i])
        for i, (source, target) in enumerate(zip(sources, targets))
    ]
    for copy in copies:
        copy.start()
    for copy in copies:
        copy.wait()


def load(*arrays):
    count = len(arrays)
    return pl.pallas_call(
        functools.partial(load_kernel, count),
        out_shape=tuple(pltpu.VMEM(a.shape, a.dtype) for a in arrays),
        in_specs=[HBM] * count,
        out_specs=(VMEM,) * count,
        scratch_shapes=[pltpu.SemaphoreType.DMA((count,))],
        compiler_params=PARAMS,
        name="load",
    )(*(pltpu.with_memory_space_constraint(a, pltpu.HBM) for a in arrays))


def project_kernel(count, *refs):
    project_rows(refs[:count], *refs[count:])


def project(strips, *params):
    rows = len(strips) * strips[0].shape[0]
    shape = pltpu.VMEM((rows, params[-1].shape[1]), jnp.bfloat16)
    return pl.pallas_call(
        functools.partial(project_kernel, len(strips)),
        out_shape=(shape, shape),
        in_specs=[VMEM] * (len(strips) + len(params)),
        out_specs=(VMEM, VMEM),
        compiler_params=PARAMS,
        name="project",
    )(*near(*strips, *params))


def attend_kernel(blocks, head_size, tile, q_ref, *refs):
    key_refs, (out_ref, scores) = refs[:blocks], refs[blocks:]
    factor = math.log2(math.e) / math.sqrt(head_size)

    def one(index):
        rows = pl.ds(pl.multiple_of(index * tile, tile), tile)
        queries = q_ref[rows, :]
        start, row_max = 0, None
        for key in key_refs:
            size = key.shape[0]
            part = lax.dot_general(
                queries, key[...], (((1,), (1,)), ((), ())), preferred_element_type=jnp.float32
            )
            scores[:, start : start + size] = part
            top = jnp.max(part, axis=-1, keepdims=True)
            row_max = top if row_max is None else jnp.maximum(row_max, top)
            start += size
        start, total, weighted = 0, None, None
        for key in key_refs:
            size = key.shape[0]
            weights = jnp.exp2((scores[:, start : start + size] - row_max) * factor)
            part_sum = jnp.sum(weights, axis=-1, keepdims=True)
            part = jnp.dot(
                weights.astype(jnp.bfloat16), key[...], preferred_element_type=jnp.float32
            )
            total = part_sum if total is None else total + part_sum
            weighted = part if weighted is None else weighted + part
            start += size
        out_ref[rows, :] = (weighted[:, head_size:] / total).astype(jnp.bfloat16)

    steps = q_ref.shape[0] // tile
    if steps == 1:
        one(0)
    else:
        lax.fori_loop(0, steps, lambda index, carry: (one(index), carry)[1], 0)


def attend(queries, keys, head_size):
    rows = queries.shape[0]
    key_count = sum(k.shape[0] for k in keys)
    tile = rows
    while tile * key_count > SCORE_BUDGET and tile % 32 == 0:
        tile //= 2
    return pl.pallas_call(
        functools.partial(attend_kernel, len(keys), head_size, tile),
        out_shape=pltpu.VMEM((rows, head_size), jnp.bfloat16),
        in_specs=[VMEM] * (1 + len(keys)),
        out_specs=VMEM,
        scratch_shapes=[pltpu.VMEM((tile, key_count), jnp.float32)],
        compiler_params=PARAMS,
        name="attend",
    )(*near(queries, *keys))


def head_rows(col_ref, mask, w_ref, head_size):
    head = jnp.bitwise_xor(col_ref[0], mask)
    return w_ref[pl.ds(pl.multiple_of(head * head_size, head_size), head_size), :]


def place_kernel(each, col_ref, *refs):
    *blocks, own, w_ref, bias, hidden, fresh_out, base_out, fresh, sent = refs
    rows, count, width, lanes = fresh.shape
    for mask in range(count):
        strip = jnp.bitwise_xor(col_ref[0], mask)
        half, at = divmod(mask * each, blocks[0].shape[0])
        fresh[:, strip] = blocks[half][at : at + each, :].reshape(rows, width, lanes)
    copy = pltpu.make_async_copy(fresh, fresh_out, sent)
    copy.start()
    product = jnp.dot(
        own[...], head_rows(col_ref, 0, w_ref, own.shape[1]), preferred_element_type=jnp.float32
    )
    base_out[...] = product + bias[...] + hidden[...].astype(jnp.float32)
    copy.wait()


def place(col, blocks, own, w_out, bias, hidden, shape):
    return pl.pallas_call(
        functools.partial(place_kernel, own.shape[0]),
        out_shape=(
            jax.ShapeDtypeStruct(shape, jnp.bfloat16),
            pltpu.VMEM(hidden.shape, jnp.float32),
        ),
        in_specs=[SMEM] + [VMEM] * (len(blocks) + 4),
        out_specs=(HBM, VMEM),
        scratch_shapes=[pltpu.VMEM(shape, jnp.bfloat16), pltpu.SemaphoreType.DMA],
        compiler_params=PARAMS,
        name="place",
    )(col, *near(*blocks, own, w_out, bias, hidden))


def finish_kernel(col_ref, base, *refs):
    *parts, w_ref, out_ref, ready, sent = refs
    head_size = parts[0].shape[1]
    rows = [head_rows(col_ref, mask, w_ref, head_size) for mask in range(1, len(parts) + 1)]
    values = [part[...] for part in parts]
    channels = base.shape[1]
    step = channels // 2 if channels % 256 == 0 else channels
    copies = []
    for index, start in enumerate(range(0, channels, step)):
        columns = slice(start, start + step)
        total = base[:, columns]
        for value, row in zip(values, rows):
            total = total + jnp.dot(
                value, row[:, columns], preferred_element_type=jnp.float32
            )
        ready[:, columns] = total.astype(jnp.bfloat16)
        copy = pltpu.make_async_copy(ready.at[:, columns], out_ref.at[:, columns], sent.at[index])
        copy.start()
        copies.append(copy)
    for copy in copies:
        copy.wait()


def finish(col, base, parts, w_out):
    return pl.pallas_call(
        finish_kernel,
        out_shape=jax.ShapeDtypeStruct(base.shape, jnp.bfloat16),
        in_specs=[SMEM] + [VMEM] * (len(parts) + 2),
        out_specs=HBM,
        scratch_shapes=[pltpu.VMEM(base.shape, jnp.bfloat16), pltpu.SemaphoreType.DMA((2,))],
        compiler_params=PARAMS,
        name="finish",
    )(col, *near(base, *parts, w_out))


def shards(hidden, ln_gain, ln_bias, w_query, w_keyval, stale_keyval, w_out, out_bias):
    band_rows, strip_cols, channels = hidden.shape
    head_size = w_query.shape[1]
    size = lax.axis_size("cols")
    half = size // 2
    each = band_rows * strip_cols
    own = hidden.reshape(each, channels)
    col = lax.axis_index("cols").astype(jnp.int32).reshape(1)
    strips = gather_by_mask(own, "cols")
    stale = gather_bands(stale_keyval.reshape(-1, 2 * head_size), "rows")[1:]
    near_own, *params = load(own, ln_gain, ln_bias, w_query.T, w_keyval)
    q_home, kv_home = project([near_own, *strips[1:half]], *params)
    q_away, kv_away = project(strips[half:], *params)
    keys = [kv_home, kv_away] + stale
    away = attend(q_away, keys, head_size)
    home = attend(q_home, keys, head_size)
    mine = {0: home[:each]}
    for mask in range(size - 1, 0, -1):
        block = away if mask >= half else home
        at = (mask % half) * each
        mine[mask] = swap(block[at : at + each], "cols", mask)
    fresh, base = place(
        col,
        [kv_home, kv_away],
        mine[0],
        w_out,
        out_bias.reshape(1, -1),
        near_own,
        (band_rows, size, strip_cols, 2 * head_size),
    )
    output = finish(col, base, [mine[m] for m in range(1, size)], w_out)
    return (
        output.reshape(hidden.shape),
        fresh.reshape(band_rows, size * strip_cols, 1, 2 * head_size),
    )


def solution(mesh):
    return jax.shard_map(
        shards,
        mesh=mesh,
        in_specs=(
            P(("groups", "rows"), "cols", None),
            P(),
            P(),
            P(None, "cols"),
            P(None, "cols"),
            P(("groups", "rows"), None, "cols", None),
            P(),
            P(),
        ),
        out_specs=(P(("groups", "rows"), "cols", None), P(("groups", "rows"), None, "cols", None)),
        check_vma=False,
    )
```

profile of v0, /device:TPU:0, one launch (start us, length us, event | category | flops | bytes accessed | tf_op | source)
XLA Modules:
  0.0 25.0 jit_solution(10046134900539550480)
XLA Ops:
  0.6 3.0 %collective-permute-start.1 = (bf16[64,1280]{1,0:T(8,128)(2,1)}, bf16[64,1280]{1,0:T(8,128)(2,1)S(1)}, u32[]{:S(2)}, u32[]{:S(2)}) collective-permute-start(bf16[64,1280]{1,0:T(8,128)(2,1)} %bitcast.9), channel_id=1, source_target_pairs={{0,2},{1,3},{2,0},{3,1},{4,6},{5,7},{6,4},{7,5},{8,10},{9,11},{10,... | collective-permute-start | bytes 491528 | tf_op jit(solution)/shard_map/ppermute | solution.py:25
  3.7 0.0 collective-permute-start
  3.7 4.4 %collective-permute-done.1.refs_0_ = bf16[64,1280]{1,0:T(8,128)(2,1)S(1)} collective-permute-done((bf16[64,1280]{1,0:T(8,128)(2,1)}, bf16[64,1280]{1,0:T(8,128)(2,1)S(1)}, u32[]{:S(2)}, u32[]{:S(2)}) %collective-permute-start.1) | collective-permute-done | bytes 163872 | tf_op jit(solution)/shard_map/ppermute | solution.py:25
  8.1 0.0 collective-permute-start.2
  8.1 1.8 %collective-permute-start.3 = (bf16[256,128]{1,0:T(8,128)(2,1)}, bf16[256,128]{1,0:T(8,128)(2,1)S(1)}, u32[]{:S(2)}, u32[]{:S(2)}) collective-permute-start(bf16[256,128]{1,0:T(8,128)(2,1)} %bitcast.13), channel_id=1, source_target_pairs={{0,4},{4,0},{8,12},{12,8},{1,5},{5,1},{9,13},{13,9},{2,6},{6,2},{1... | collective-permute-start | bytes 196616 | tf_op jit(solution)/shard_map/ppermute | solution.py:25
  9.9 2.6 %collective-permute-start.4 = (bf16[256,128]{1,0:T(8,128)(2,1)}, bf16[256,128]{1,0:T(8,128)(2,1)S(1)}, u32[]{:S(2)}, u32[]{:S(2)}) collective-permute-start(bf16[256,128]{1,0:T(8,128)(2,1)} %bitcast.14), channel_id=1, source_target_pairs={{0,8},{4,12},{8,0},{12,4},{1,9},{5,13},{9,1},{13,5},{2,10},{6,14},... | collective-permute-start | bytes 196616 | tf_op jit(solution)/shard_map/ppermute | solution.py:25
  12.5 0.0 collective-permute-start.5
  12.5 1.2 %load.1 = (bf16[64,1280]{1,0:T(8,128)(2,1)S(1)}, f32[1280]{0:T(1024)S(1)}, f32[1280]{0:T(1024)S(1)}, bf16[64,1280]{1,0:T(8,128)(2,1)S(1)}, bf16[1280,128]{1,0:T(8,128)(2,1)S(1)}) custom-call(bf16[64,1280]{1,0:T(8,128)(2,1)} %bitcast.11, f32[1280]{0:T(1024)} %refs_1_.1, f32[1280]{0:T(1024)} %refs_2_.1, bf16[64,1280]{1,0:T(8,128)(2,1)} %bitcast.8, ...), custom_call_target="tpu_custom_call" | custom-call | tf_op jit(solution)/shard_map/load/pallas_call | solution.py:82
  13.7 0.0 collective-permute-done.refs_1_
  13.7 0.6 %project.2 = (bf16[128,128]{1,0:T(8,128)(2,1)S(1)}, bf16[128,128]{1,0:T(8,128)(2,1)S(1)}) custom-call(bf16[64,1280]{1,0:T(8,128)(2,1)S(1)} %get-tuple-element.13.refs_0_.refs_5_, bf16[64,1280]{1,0:T(8,128)(2,1)S(1)} %collective-permute-done.refs_1_, f32[1280]{0:T(1024)S(1)} %get-tuple-element.14.refs_2_, f32[1280]{0:T(1024)S(1)} %get-tuple-element.15.refs_3_, ...), custom_call_target="tpu_custom_call" | custom-call | tf_op jit(solution)/shard_map/project/pallas_call | solution.py:100
  14.3 0.0 copy-start
  14.3 0.0 collective-permute-done.2.refs_1_
  14.3 0.6 %project.3 = (bf16[128,128]{1,0:T(8,128)(2,1)S(1)}, bf16[128,128]{1,0:T(8,128)(2,1)S(1)}) custom-call(bf16[64,1280]{1,0:T(8,128)(2,1)S(1)} %collective-permute-done.1.refs_0_, bf16[64,1280]{1,0:T(8,128)(2,1)S(1)} %collective-permute-done.2.refs_1_, f32[1280]{0:T(1024)S(1)} %get-tuple-element.14.refs_2_, f32[1280]{0:T(1024)S(1)} %get-tuple-element.15.refs_3_, ...), custom_call_target="tpu_custom_call" | custom-call | tf_op jit(solution)/shard_map/project/pallas_call | solution.py:100
  14.9 0.0 collective-permute-done.3.refs_2_
  14.9 2.2 %collective-permute-done.4.refs_3_ = bf16[256,128]{1,0:T(8,128)(2,1)S(1)} collective-permute-done((bf16[256,128]{1,0:T(8,128)(2,1)}, bf16[256,128]{1,0:T(8,128)(2,1)S(1)}, u32[]{:S(2)}, u32[]{:S(2)}) %collective-permute-start.4) | collective-permute-done | bytes 65568 | tf_op jit(solution)/shard_map/ppermute | solution.py:25
  17.1 1.7 %collective-permute-done.5.refs_4_ = bf16[256,128]{1,0:T(8,128)(2,1)S(1)} collective-permute-done((bf16[256,128]{1,0:T(8,128)(2,1)}, bf16[256,128]{1,0:T(8,128)(2,1)S(1)}, u32[]{:S(2)}, u32[]{:S(2)}) %collective-permute-start.5) | collective-permute-done | bytes 65568 | tf_op jit(solution)/shard_map/ppermute | solution.py:25
  18.8 0.6 %attend.3 = bf16[128,64]{1,0:T(8,128)(2,1)S(1)} custom-call(bf16[128,128]{1,0:T(8,128)(2,1)S(1)} %get-tuple-element.22.q_ref, bf16[128,128]{1,0:T(8,128)(2,1)S(1)} %get-tuple-element.18.refs_0_, bf16[128,128]{1,0:T(8,128)(2,1)S(1)} %get-tuple-element.19.refs_1_, bf16[256,128]{1,0:T(8,128)(2,1)S(1)} %collective-permute-done.3.refs_2_, ...), custom_call_target="tpu_custom_call" | custom-call | tf_op jit(solution)/shard_map/attend/pallas_call | solution.py:153
  19.4 1.6 %collective-permute-start.7 = (bf16[64,64]{1,0:T(8,128)(2,1)S(1)}, bf16[64,64]{1,0:T(8,128)(2,1)S(1)}, u32[]{:S(2)}, u32[]{:S(2)}) collective-permute-start(bf16[64,64]{1,0:T(8,128)(2,1)S(1)} %get-tuple-element.27), channel_id=1, source_target_pairs={{0,2},{1,3},{2,0},{3,1},{4,6},{5,7},{6,4},{7,5},{8,10},{9,11},{10,... | collective-permute-start | bytes 24584 | tf_op jit(solution)/shard_map/ppermute | solution.py:25
  20.9 0.0 collective-permute-start.8
  20.9 0.6 %attend.2 = bf16[128,64]{1,0:T(8,128)(2,1)S(1)} custom-call(bf16[128,128]{1,0:T(8,128)(2,1)S(1)} %get-tuple-element.20.q_ref, bf16[128,128]{1,0:T(8,128)(2,1)S(1)} %get-tuple-element.18.refs_0_, bf16[128,128]{1,0:T(8,128)(2,1)S(1)} %get-tuple-element.19.refs_1_, bf16[256,128]{1,0:T(8,128)(2,1)S(1)} %collective-permute-done.3.refs_2_, ...), custom_call_target="tpu_custom_call" | custom-call | tf_op jit(solution)/shard_map/attend/pallas_call | solution.py:153
  21.6 0.0 copy-start.1
  21.6 0.7 %collective-permute-start.6 = (bf16[64,64]{1,0:T(8,128)(2,1)S(1)}, bf16[64,64]{1,0:T(8,128)(2,1)S(1)}, u32[]{:S(2)}, u32[]{:S(2)}) collective-permute-start(bf16[64,64]{1,0:T(8,128)(2,1)S(1)} %get-tuple-element.28), channel_id=1, source_target_pairs={{0,1},{1,0},{2,3},{3,2},{4,5},{5,4},{6,7},{7,6},{8,9},{9,8},{10,11... | collective-permute-start | bytes 24584 | tf_op jit(solution)/shard_map/ppermute | solution.py:25
  22.3 0.0 copy-done.1
  22.3 0.0 copy-done
  22.3 0.7 %place.1 = (bf16[8,4,8,128]{3,2,1,0:T(8,128)(2,1)}, f32[64,1280]{1,0:T(8,128)S(1)}) custom-call(s32[1]{0:T(128)} %bitcast.col_ref, bf16[128,128]{1,0:T(8,128)(2,1)S(1)} %get-tuple-element.18.refs_0_, bf16[128,128]{1,0:T(8,128)(2,1)S(1)} %get-tuple-element.19.refs_1_, bf16[64,64]{1,0:T(8,128)(2,1)S(1)} %get-tuple-element.29.refs_2_, ...), custom_call_target="tpu_custom_call" | custom-call | tf_op jit(solution)/shard_map/place/pallas_call | solution.py:186
  23.0 0.2 collective-permute-done.7.refs_1_
  23.2 0.9 %collective-permute-done.8.refs_2_ = bf16[64,64]{1,0:T(8,128)(2,1)S(1)} collective-permute-done((bf16[64,64]{1,0:T(8,128)(2,1)S(1)}, bf16[64,64]{1,0:T(8,128)(2,1)S(1)}, u32[]{:S(2)}, u32[]{:S(2)}) %collective-permute-start.8) | collective-permute-done | bytes 8224 | tf_op jit(solution)/shard_map/ppermute | solution.py:25
  24.1 0.0 collective-permute-done.6.refs_0_
  24.1 0.9 %finish.1 = bf16[64,1280]{1,0:T(8,128)(2,1)} custom-call(s32[1]{0:T(128)} %bitcast.col_ref, f32[64,1280]{1,0:T(8,128)S(1)} %get-tuple-element.21.base, bf16[64,64]{1,0:T(8,128)(2,1)S(1)} %collective-permute-done.6.refs_0_, bf16[64,64]{1,0:T(8,128)(2,1)S(1)} %collective-permute-done.7.refs_1_, bf16[64,64]{1,0:T(8,128)(2,1)S(1)} %collective-permute-done.8.refs_2_, ...), custom_call_target="tpu_custom_call" | custom-call | tf_op jit(solution)/shard_map/finish/pallas_call | solution.py:224
  (3 shorter events, 0.0 us)
Async XLA Ops:
  0.6 7.4 %collective-permute-start.1 = (bf16[64,1280]{1,0:T(8,128)(2,1)}, bf16[64,1280]{1,0:T(8,128)(2,1)S(1)}, u32[]{:S(2)}, u32[]{:S(2)}) collective-permute-start(bf16[64,1280]{1,0:T(8,128)(2,1)} %bitcast.9), channel_id=1, source_target_pairs={{0,2},{1,3},{2,0},{3,1},{4,6},{5,7},{6,4},{7,5},{8,10},{9,11},{10,... | collective-permute-start | bytes 491528 | tf_op jit(solution)/shard_map/ppermute | solution.py:25
  3.7 10.1 %collective-permute-start = (bf16[64,1280]{1,0:T(8,128)(2,1)}, bf16[64,1280]{1,0:T(8,128)(2,1)S(1)}, u32[]{:S(2)}, u32[]{:S(2)}) collective-permute-start(bf16[64,1280]{1,0:T(8,128)(2,1)} %bitcast.10), channel_id=1, source_target_pairs={{0,1},{1,0},{2,3},{3,2},{4,5},{5,4},{6,7},{7,6},{8,9},{9,8},{10,11... | collective-permute-start | bytes 491528 | tf_op jit(solution)/shard_map/ppermute | solution.py:25
  8.1 6.2 %collective-permute-start.2 = (bf16[64,1280]{1,0:T(8,128)(2,1)S(1)}, bf16[64,1280]{1,0:T(8,128)(2,1)S(1)}, u32[]{:S(2)}, u32[]{:S(2)}) collective-permute-start(bf16[64,1280]{1,0:T(8,128)(2,1)S(1)} %collective-permute-done.1.refs_0_), channel_id=1, source_target_pairs={{0,1},{1,0},{2,3},{3,2},{4,5},{5,4},{6,7},{7,6},{8,9},{9,8},{10,11... | collective-permute-start | bytes 491528 | tf_op jit(solution)/shard_map/ppermute | solution.py:25
  8.1 6.8 %collective-permute-start.3 = (bf16[256,128]{1,0:T(8,128)(2,1)}, bf16[256,128]{1,0:T(8,128)(2,1)S(1)}, u32[]{:S(2)}, u32[]{:S(2)}) collective-permute-start(bf16[256,128]{1,0:T(8,128)(2,1)} %bitcast.13), channel_id=1, source_target_pairs={{0,4},{4,0},{8,12},{12,8},{1,5},{5,1},{9,13},{13,9},{2,6},{6,2},{1... | collective-permute-start | bytes 196616 | tf_op jit(solution)/shard_map/ppermute | solution.py:25
  9.9 7.2 %collective-permute-start.4 = (bf16[256,128]{1,0:T(8,128)(2,1)}, bf16[256,128]{1,0:T(8,128)(2,1)S(1)}, u32[]{:S(2)}, u32[]{:S(2)}) collective-permute-start(bf16[256,128]{1,0:T(8,128)(2,1)} %bitcast.14), channel_id=1, source_target_pairs={{0,8},{4,12},{8,0},{12,4},{1,9},{5,13},{9,1},{13,5},{2,10},{6,14},... | collective-permute-start | bytes 196616 | tf_op jit(solution)/shard_map/ppermute | solution.py:25
  12.5 6.3 %collective-permute-start.5 = (bf16[256,128]{1,0:T(8,128)(2,1)}, bf16[256,128]{1,0:T(8,128)(2,1)S(1)}, u32[]{:S(2)}, u32[]{:S(2)}) collective-permute-start(bf16[256,128]{1,0:T(8,128)(2,1)} %bitcast.15), channel_id=1, source_target_pairs={{0,12},{4,8},{8,4},{12,0},{1,13},{5,9},{9,5},{13,1},{2,14},{6,10},... | collective-permute-start | bytes 196616 | tf_op jit(solution)/shard_map/ppermute | solution.py:25
  14.3 8.0 %copy-start = (bf16[256,1280]{1,0:T(8,128)(2,1)S(1)}, bf16[256,1280]{1,0:T(8,128)(2,1)}, u32[]{:S(2)}) copy-start(bf16[256,1280]{1,0:T(8,128)(2,1)} %refs_3_.3) | copy-start | bytes 1966084
  19.4 3.8 %collective-permute-start.7 = (bf16[64,64]{1,0:T(8,128)(2,1)S(1)}, bf16[64,64]{1,0:T(8,128)(2,1)S(1)}, u32[]{:S(2)}, u32[]{:S(2)}) collective-permute-start(bf16[64,64]{1,0:T(8,128)(2,1)S(1)} %get-tuple-element.27), channel_id=1, source_target_pairs={{0,2},{1,3},{2,0},{3,1},{4,6},{5,7},{6,4},{7,5},{8,10},{9,11},{10,... | collective-permute-start | bytes 24584 | tf_op jit(solution)/shard_map/ppermute | solution.py:25
  20.9 3.2 %collective-permute-start.8 = (bf16[64,64]{1,0:T(8,128)(2,1)S(1)}, bf16[64,64]{1,0:T(8,128)(2,1)S(1)}, u32[]{:S(2)}, u32[]{:S(2)}) collective-permute-start(bf16[64,64]{1,0:T(8,128)(2,1)S(1)} %get-tuple-element.26), channel_id=1, source_target_pairs={{0,3},{1,2},{2,1},{3,0},{4,7},{5,6},{6,5},{7,4},{8,11},{9,10},{10,... | collective-permute-start | bytes 24584 | tf_op jit(solution)/shard_map/ppermute | solution.py:25
  21.6 0.7 %copy-start.1 = (f32[1280]{0:T(1024)S(1)}, f32[1280]{0:T(1024)}, u32[]{:S(2)}) copy-start(f32[1280]{0:T(1024)} %param.15) | copy-start | bytes 15364
  21.6 2.5 %collective-permute-start.6 = (bf16[64,64]{1,0:T(8,128)(2,1)S(1)}, bf16[64,64]{1,0:T(8,128)(2,1)S(1)}, u32[]{:S(2)}, u32[]{:S(2)}) collective-permute-start(bf16[64,64]{1,0:T(8,128)(2,1)S(1)} %get-tuple-element.28), channel_id=1, source_target_pairs={{0,1},{1,0},{2,3},{3,2},{4,5},{5,4},{6,7},{7,6},{8,9},{9,8},{10,11... | collective-permute-start | bytes 24584 | tf_op jit(solution)/shard_map/ppermute | solution.py:25
where the time goes:
time: 25.2 us; the launch traced here: 25 us
  starting transfers between devices  9.72 us (39%)
  waiting for transfers between devices  9.39 us (37%)
  Pallas kernels  5.19 us (21%)
  between operations  0.72 us (3%)
    ppermute x9, starting transfers between devices, swap(): return lax.ppermute(block, axis, [(i, i ^ mask) for i in range(size)])  9.72 us
    ppermute x9, waiting for transfers between devices, swap(): return lax.ppermute(block, axis, [(i, i ^ mask) for i in range(size)])  9.39 us
    pallas_call x2, Pallas kernels, attend(): pl.pallas_call(functools.partial(attend_kernel, len(keys), head_size, til...  1.23 us
    pallas_call x1, Pallas kernels, load(): pl.pallas_call(functools.partial(load_kernel, count), out_shape=tuple((pl...  1.21 us
    pallas_call x2, Pallas kernels, project(): pl.pallas_call(functools.partial(project_kernel, len(strips)), out_shape=...  1.1 us
    pallas_call x1, Pallas kernels, finish(): pl.pallas_call(finish_kernel, out_shape=jax.ShapeDtypeStruct(base.shape,...  0.93 us
    pallas_call x1, Pallas kernels, place(): pl.pallas_call(functools.partial(place_kernel, own.shape[0]), out_shape=(...  0.71 us
  transfers between devices with their start and end apart: 9, of which 5 were waited for; matrix products, arithmetic and copies ran while one was open for 0% of the time, Pallas kernels for 15%

commit v1 on v0

--- a/solution.py
+++ b/solution.py
@@ -34,7 +34,11 @@
 
 
 def gather_bands(block, axis):
-    return [block] + [swap(block, axis, m) for m in range(1, lax.axis_size(axis))]
+    size = lax.axis_size(axis)
+    blocks = []
+    for step in range(1, size):
+        blocks.append(lax.ppermute(block, axis, [(i, (i + step) % size) for i in range(size)]))
+    return blocks
 
 
 def gather_by_mask(block, axis):
@@ -107,12 +111,10 @@
     )(*near(*strips, *params))
 
 
-def attend_kernel(blocks, head_size, tile, q_ref, *refs):
-    key_refs, (out_ref, scores) = refs[:blocks], refs[blocks:]
+def attend_rows(head_size, tile, q_ref, key_refs, out_ref, scores):
     factor = math.log2(math.e) / math.sqrt(head_size)
 
-    def one(index):
-        rows = pl.ds(pl.multiple_of(index * tile, tile), tile)
+    def one(rows):
         queries = q_ref[rows, :]
         start, row_max = 0, None
         for key in key_refs:
@@ -139,26 +141,79 @@
 
     steps = q_ref.shape[0] // tile
     if steps == 1:
-        one(0)
+        one(pl.ds(0, tile))
     else:
-        lax.fori_loop(0, steps, lambda index, carry: (one(index), carry)[1], 0)
-
-
-def attend(queries, keys, head_size):
-    rows = queries.shape[0]
+
+        def step(index, carry):
+            one(pl.ds(pl.multiple_of(index * tile, tile), tile))
+            return carry
+
+        lax.fori_loop(0, steps, step, 0)
+
+
+def score_tile(rows, keys):
     key_count = sum(k.shape[0] for k in keys)
     tile = rows
     while tile * key_count > SCORE_BUDGET and tile % 32 == 0:
         tile //= 2
-    return pl.pallas_call(
-        functools.partial(attend_kernel, len(keys), head_size, tile),
+    return tile, pltpu.VMEM((tile, key_count), jnp.float32)
+
+
+def away_kernel(blocks, head_size, tile, q_ref, *refs):
+    attend_rows(head_size, tile, q_ref, refs[:blocks], *refs[blocks:])
+
+
+def attend_away(queries, keys, head_size):
+    rows = queries.shape[0]
+    tile, scores = score_tile(rows, keys)
+    return pl.pallas_call(
+        functools.partial(away_kernel, len(keys), head_size, tile),
         out_shape=pltpu.VMEM((rows, head_size), jnp.bfloat16),
         in_specs=[VMEM] * (1 + len(keys)),
         out_specs=VMEM,
-        scratch_shapes=[pltpu.VMEM((tile, key_count), jnp.float32)],
-        compiler_params=PARAMS,
-        name="attend",
+        scratch_shapes=[scores],
+        compiler_params=PARAMS,
+        name="attend_away",
     )(*near(queries, *keys))
+
+
+def home_kernel(blocks, head_size, tile, col_ref, q_ref, *refs):
+    keys, (out_ref, fresh_out, scores, fresh, sent) = refs[:blocks], refs[blocks:]
+    rows, count, width, lanes = fresh.shape
+    each = rows * width
+    for mask in range(count):
+        strip = jnp.bitwise_xor(col_ref[0], mask)
+        half, at = divmod(mask * each, keys[0].shape[0])
+        fresh[:, strip] = keys[half][at : at + each, :].reshape(rows, width, lanes)
+    copy = pltpu.make_async_copy(fresh, fresh_out, sent)
+    copy.start()
+
+    @pl.when(col_ref[0] >= 0)
+    def _():
+        attend_rows(head_size, tile, q_ref, keys, out_ref, scores)
+
+    copy.wait()
+
+
+def attend_home(col, queries, keys, head_size, fresh_shape):
+    rows = queries.shape[0]
+    tile, scores = score_tile(rows, keys)
+    return pl.pallas_call(
+        functools.partial(home_kernel, len(keys), head_size, tile),
+        out_shape=(
+            pltpu.VMEM((rows, head_size), jnp.bfloat16),
+            jax.ShapeDtypeStruct(fresh_shape, jnp.bfloat16),
+        ),
+        in_specs=[SMEM] + [VMEM] * (1 + len(keys)),
+        out_specs=(VMEM, HBM),
+        scratch_shapes=[
+            scores,
+            pltpu.VMEM(fresh_shape, jnp.bfloat16),
+            pltpu.SemaphoreType.DMA,
+        ],
+        compiler_params=PARAMS,
+        name="attend_home",
+    )(col, *near(queries, *keys))
 
 
 def head_rows(col_ref, mask, w_ref, head_size):
@@ -166,35 +221,23 @@
     return w_ref[pl.ds(pl.multiple_of(head * head_size, head_size), head_size), :]
 
 
-def place_kernel(each, col_ref, *refs):
-    *blocks, own, w_ref, bias, hidden, fresh_out, base_out, fresh, sent = refs
-    rows, count, width, lanes = fresh.shape
-    for mask in range(count):
-        strip = jnp.bitwise_xor(col_ref[0], mask)
-        half, at = divmod(mask * each, blocks[0].shape[0])
-        fresh[:, strip] = blocks[half][at : at + each, :].reshape(rows, width, lanes)
-    copy = pltpu.make_async_copy(fresh, fresh_out, sent)
-    copy.start()
+def begin_kernel(col_ref, home, w_ref, bias, hidden, out_ref):
+    own = home[: hidden.shape[0], :]
     product = jnp.dot(
-        own[...], head_rows(col_ref, 0, w_ref, own.shape[1]), preferred_element_type=jnp.float32
-    )
-    base_out[...] = product + bias[...] + hidden[...].astype(jnp.float32)
-    copy.wait()
-
-
-def place(col, blocks, own, w_out, bias, hidden, shape):
-    return pl.pallas_call(
-        functools.partial(place_kernel, own.shape[0]),
-        out_shape=(
-            jax.ShapeDtypeStruct(shape, jnp.bfloat16),
-            pltpu.VMEM(hidden.shape, jnp.float32),
-        ),
-        in_specs=[SMEM] + [VMEM] * (len(blocks) + 4),
-        out_specs=(HBM, VMEM),
-        scratch_shapes=[pltpu.VMEM(shape, jnp.bfloat16), pltpu.SemaphoreType.DMA],
-        compiler_params=PARAMS,
-        name="place",
-    )(col, *near(*blocks, own, w_out, bias, hidden))
+        own, head_rows(col_ref, 0, w_ref, own.shape[1]), preferred_element_type=jnp.float32
+    )
+    out_ref[...] = product + bias[...].reshape(1, -1) + hidden[...].astype(jnp.float32)
+
+
+def begin(col, home, w_out, bias, hidden):
+    return pl.pallas_call(
+        begin_kernel,
+        out_shape=pltpu.VMEM(hidden.shape, jnp.float32),
+        in_specs=[SMEM] + [VMEM] * 4,
+        out_specs=VMEM,
+        compiler_params=PARAMS,
+        name="begin",
+    )(col, *near(home, w_out, bias, hidden))
 
 
 def finish_kernel(col_ref, base, *refs):
@@ -241,28 +284,23 @@
     own = hidden.reshape(each, channels)
     col = lax.axis_index("cols").astype(jnp.int32).reshape(1)
     strips = gather_by_mask(own, "cols")
-    stale = gather_bands(stale_keyval.reshape(-1, 2 * head_size), "rows")[1:]
-    near_own, *params = load(own, ln_gain, ln_bias, w_query.T, w_keyval)
+    stale = gather_bands(stale_keyval.reshape(-1, 2 * head_size), "rows")
+    near_own, near_out, near_bias, *params = load(
+        own, w_out, out_bias, ln_gain, ln_bias, w_query.T, w_keyval
+    )
     q_home, kv_home = project([near_own, *strips[1:half]], *params)
     q_away, kv_away = project(strips[half:], *params)
     keys = [kv_home, kv_away] + stale
-    away = attend(q_away, keys, head_size)
-    home = attend(q_home, keys, head_size)
-    mine = {0: home[:each]}
+    away = attend_away(q_away, keys, head_size)
+    fresh_shape = (band_rows, size, strip_cols, 2 * head_size)
+    home, fresh = attend_home(col, q_home, keys, head_size, fresh_shape)
+    mine = {}
     for mask in range(size - 1, 0, -1):
         block = away if mask >= half else home
         at = (mask % half) * each
         mine[mask] = swap(block[at : at + each], "cols", mask)
-    fresh, base = place(
-        col,
-        [kv_home, kv_away],
-        mine[0],
-        w_out,
-        out_bias.reshape(1, -1),
-        near_own,
-        (band_rows, size, strip_cols, 2 * head_size),
-    )
-    output = finish(col, base, [mine[m] for m in range(1, size)], w_out)
+    base = begin(col, home, near_out, near_bias, near_own)
+    output = finish(col, base, [mine[m] for m in range(1, size)], near_out)
     return (
         output.reshape(hidden.shape),
         fresh.reshape(band_rows, size * strip_cols, 1, 2 * head_size),

time: 25.2 us -> 24.5 us (0.972)
  waiting for transfers between devices: 9.39 us -> 7.62 us
  starting transfers between devices: 9.72 us -> 11.1 us
  Pallas kernels: 5.19 us -> 4.91 us
    ppermute x0 -> x3, starting transfers between devices: none -> 5.76 us  [gather_bands(): lax.ppermute(block, axis, [(i, (i + step) % size) for i in range(size)])]
    ppermute x9 -> x6, starting transfers between devices: 9.72 us -> 5.31 us  [swap(): return lax.ppermute(block, axis, [(i, i ^ mask) for i in range(size)])]
    ppermute x9 -> x6, waiting for transfers between devices: 9.39 us -> 6 us  [swap(): return lax.ppermute(block, axis, [(i, i ^ mask) for i in range(size)])]
    ppermute x0 -> x3, waiting for transfers between devices: none -> 1.61 us  [gather_bands(): lax.ppermute(block, axis, [(i, (i + step) % size) for i in range(size)])]
    pallas_call x3, Pallas kernels: 1.94 us -> 1.44 us  [the longest x1 0.65 us: attend_home(): pl.pallas_call(functools.partial(home_kernel, len(keys), head_size, tile)...]
  transfers between devices with their start and end apart: 9 -> 9, of which waited for: 5 -> 5; matrix products, arithmetic and copies ran while one was open for 0% -> 0% of each run, Pallas kernels for 15% -> 14%
where the time goes in v1:
time: 24.5 us; the launch traced here: 24.3 us
  starting transfers between devices  11.1 us (45%)
  waiting for transfers between devices  7.62 us (31%)
  Pallas kernels  4.91 us (20%)
  between operations  0.71 us (3%)
    ppermute x6, waiting for transfers between devices, swap(): return lax.ppermute(block, axis, [(i, i ^ mask) for i in range(size)])  6 us
    ppermute x3, starting transfers between devices, gather_bands(): lax.ppermute(block, axis, [(i, (i + step) % size) for i in range(size)])  5.76 us
    ppermute x6, starting transfers between devices, swap(): return lax.ppermute(block, axis, [(i, i ^ mask) for i in range(size)])  5.31 us
    ppermute x3, waiting for transfers between devices, gather_bands(): lax.ppermute(block, axis, [(i, (i + step) % size) for i in range(size)])  1.61 us
    pallas_call x1, Pallas kernels, load(): pl.pallas_call(functools.partial(load_kernel, count), out_shape=tuple((pl...  1.41 us
    pallas_call x2, Pallas kernels, project(): pl.pallas_call(functools.partial(project_kernel, len(strips)), out_shape=...  1.12 us
    pallas_call x1, Pallas kernels, finish(): pl.pallas_call(finish_kernel, out_shape=jax.ShapeDtypeStruct(base.shape,...  0.93 us
    pallas_call x1, Pallas kernels, attend_home(): pl.pallas_call(functools.partial(home_kernel, len(keys), head_size, tile)...  0.65 us
  transfers between devices with their start and end apart: 9, of which 5 were waited for; matrix products, arithmetic and copies ran while one was open for 0% of the time, Pallas kernels for 14%

profile of v1, /device:TPU:0, one launch (start us, length us, event | category | flops | bytes accessed | tf_op | source)
XLA Modules:
  0.0 24.3 jit_solution(17359772252901853093)
XLA Ops:
  0.6 3.0 %collective-permute-start.1 = (bf16[64,1280]{1,0:T(8,128)(2,1)}, bf16[64,1280]{1,0:T(8,128)(2,1)S(1)}, u32[]{:S(2)}, u32[]{:S(2)}) collective-permute-start(bf16[64,1280]{1,0:T(8,128)(2,1)} %bitcast.9), channel_id=1, source_target_pairs={{0,2},{1,3},{2,0},{3,1},{4,6},{5,7},{6,4},{7,5},{8,10},{9,11},{10,... | collective-permute-start | bytes 491528 | tf_op jit(solution)/shard_map/ppermute | solution.py:25
  3.7 0.0 collective-permute-start
  3.7 4.4 %collective-permute-done.1.refs_0_ = bf16[64,1280]{1,0:T(8,128)(2,1)S(1)} collective-permute-done((bf16[64,1280]{1,0:T(8,128)(2,1)}, bf16[64,1280]{1,0:T(8,128)(2,1)S(1)}, u32[]{:S(2)}, u32[]{:S(2)}) %collective-permute-start.1) | collective-permute-done | bytes 163872 | tf_op jit(solution)/shard_map/ppermute | solution.py:25
  8.1 0.0 collective-permute-start.2
  8.1 1.8 %collective-permute-start.3 = (bf16[256,128]{1,0:T(8,128)(2,1)}, bf16[256,128]{1,0:T(8,128)(2,1)S(1)}, u32[]{:S(2)}, u32[]{:S(2)}) collective-permute-start(bf16[256,128]{1,0:T(8,128)(2,1)} %bitcast.13), channel_id=1, source_target_pairs={{0,4},{4,8},{8,12},{12,0},{1,5},{5,9},{9,13},{13,1},{2,6},{6,10},{... | collective-permute-start | bytes 196616 | tf_op jit(solution)/shard_map/ppermute | solution.py:40
  9.9 2.6 %collective-permute-start.4 = (bf16[256,128]{1,0:T(8,128)(2,1)}, bf16[256,128]{1,0:T(8,128)(2,1)S(1)}, u32[]{:S(2)}, u32[]{:S(2)}) collective-permute-start(bf16[256,128]{1,0:T(8,128)(2,1)} %bitcast.14), channel_id=1, source_target_pairs={{0,8},{4,12},{8,0},{12,4},{1,9},{5,13},{9,1},{13,5},{2,10},{6,14},... | collective-permute-start | bytes 196616 | tf_op jit(solution)/shard_map/ppermute | solution.py:40
  12.5 1.3 %collective-permute-start.5 = (bf16[256,128]{1,0:T(8,128)(2,1)}, bf16[256,128]{1,0:T(8,128)(2,1)S(1)}, u32[]{:S(2)}, u32[]{:S(2)}) collective-permute-start(bf16[256,128]{1,0:T(8,128)(2,1)} %bitcast.15), channel_id=1, source_target_pairs={{0,12},{4,0},{8,4},{12,8},{1,13},{5,1},{9,5},{13,9},{2,14},{6,2},{... | collective-permute-start | bytes 196616 | tf_op jit(solution)/shard_map/ppermute | solution.py:40
  13.8 1.4 %load.1 = (bf16[64,1280]{1,0:T(8,128)(2,1)S(1)}, bf16[256,1280]{1,0:T(8,128)(2,1)S(1)}, f32[1280]{0:T(1024)S(1)}, f32[1280]{0:T(1024)S(1)}, f32[1280]{0:T(1024)S...) custom-call(bf16[64,1280]{1,0:T(8,128)(2,1)} %bitcast.11, bf16[256,1280]{1,0:T(8,128)(2,1)} %refs_1_.1, ...), custom_call_target="tpu_custom_call" | custom-call | tf_op jit(solution)/shard_map/load/pallas_call | solution.py:86
  15.3 0.0 collective-permute-done.refs_1_
  15.3 0.6 %project.2 = (bf16[128,128]{1,0:T(8,128)(2,1)S(1)}, bf16[128,128]{1,0:T(8,128)(2,1)S(1)}) custom-call(bf16[64,1280]{1,0:T(8,128)(2,1)S(1)} %get-tuple-element.15.refs_0_.hidden, bf16[64,1280]{1,0:T(8,128)(2,1)S(1)} %collective-permute-done.refs_1_, f32[1280]{0:T(1024)S(1)} %get-tuple-element.16.refs_2_, f32[1280]{0:T(1024)S(1)} %get-tuple-element.17.refs_3_, ...), custom_call_target="tpu_custom_call" | custom-call | tf_op jit(solution)/shard_map/project/pallas_call | solution.py:104
  15.8 0.0 collective-permute-done.2.refs_1_
  15.9 0.6 %project.3 = (bf16[128,128]{1,0:T(8,128)(2,1)S(1)}, bf16[128,128]{1,0:T(8,128)(2,1)S(1)}) custom-call(bf16[64,1280]{1,0:T(8,128)(2,1)S(1)} %collective-permute-done.1.refs_0_, bf16[64,1280]{1,0:T(8,128)(2,1)S(1)} %collective-permute-done.2.refs_1_, f32[1280]{0:T(1024)S(1)} %get-tuple-element.16.refs_2_, f32[1280]{0:T(1024)S(1)} %get-tuple-element.17.refs_3_, ...), custom_call_target="tpu_custom_call" | custom-call | tf_op jit(solution)/shard_map/project/pallas_call | solution.py:104
  16.4 0.0 collective-permute-done.3.refs_2_
  16.4 1.4 %collective-permute-done.4.refs_3_ = bf16[256,128]{1,0:T(8,128)(2,1)S(1)} collective-permute-done((bf16[256,128]{1,0:T(8,128)(2,1)}, bf16[256,128]{1,0:T(8,128)(2,1)S(1)}, u32[]{:S(2)}, u32[]{:S(2)}) %collective-permute-start.4) | collective-permute-done | bytes 65568 | tf_op jit(solution)/shard_map/ppermute | solution.py:40
  17.8 0.2 collective-permute-done.5.refs_4_
  18.0 0.6 %attend_away.1 = bf16[128,64]{1,0:T(8,128)(2,1)S(1)} custom-call(bf16[128,128]{1,0:T(8,128)(2,1)S(1)} %get-tuple-element.26.q_ref, bf16[128,128]{1,0:T(8,128)(2,1)S(1)} %get-tuple-element.21.refs_0_, bf16[128,128]{1,0:T(8,128)(2,1)S(1)} %get-tuple-element.22.refs_1_, bf16[256,128]{1,0:T(8,128)(2,1)S(1)} %collective-permute-done.3.refs_2_, ...), custom_call_target="tpu_custom_call" | custom-call | tf_op jit(solution)/shard_map/attend_away/pallas_call | solution.py:169
  18.7 1.6 %collective-permute-start.7 = (bf16[64,64]{1,0:T(8,128)(2,1)S(1)}, bf16[64,64]{1,0:T(8,128)(2,1)S(1)}, u32[]{:S(2)}, u32[]{:S(2)}) collective-permute-start(bf16[64,64]{1,0:T(8,128)(2,1)S(1)} %get-tuple-element.31), channel_id=1, source_target_pairs={{0,2},{1,3},{2,0},{3,1},{4,6},{5,7},{6,4},{7,5},{8,10},{9,11},{10,... | collective-permute-start | bytes 24584 | tf_op jit(solution)/shard_map/ppermute | solution.py:25
  20.2 0.0 collective-permute-start.8
  20.2 0.6 %attend_home.1 = (bf16[128,64]{1,0:T(8,128)(2,1)S(1)}, bf16[8,4,8,128]{3,2,1,0:T(8,128)(2,1)}) custom-call(s32[1]{0:T(128)} %bitcast.col_ref, bf16[128,128]{1,0:T(8,128)(2,1)S(1)} %get-tuple-element.20.q_ref, bf16[128,128]{1,0:T(8,128)(2,1)S(1)} %get-tuple-element.21.refs_0_, bf16[128,128]{1,0:T(8,128)(2,1)S(1)} %get-tuple-element.22.refs_1_, ...), custom_call_target="tpu_custom_call" | custom-call | tf_op jit(solution)/shard_map/attend_home/pallas_call | solution.py:201
  20.9 0.7 %collective-permute-start.6 = (bf16[64,64]{1,0:T(8,128)(2,1)S(1)}, bf16[64,64]{1,0:T(8,128)(2,1)S(1)}, u32[]{:S(2)}, u32[]{:S(2)}) collective-permute-start(bf16[64,64]{1,0:T(8,128)(2,1)S(1)} %slice.9), channel_id=1, source_target_pairs={{0,1},{1,0},{2,3},{3,2},{4,5},{5,4},{6,7},{7,6},{8,9},{9,8},{10,11... | collective-permute-start | bytes 24584 | tf_op jit(solution)/shard_map/ppermute | solution.py:25
  21.6 0.2 begin.1.base
  21.8 0.7 %collective-permute-done.7.refs_1_ = bf16[64,64]{1,0:T(8,128)(2,1)S(1)} collective-permute-done((bf16[64,64]{1,0:T(8,128)(2,1)S(1)}, bf16[64,64]{1,0:T(8,128)(2,1)S(1)}, u32[]{:S(2)}, u32[]{:S(2)}) %collective-permute-start.7) | collective-permute-done | bytes 8224 | tf_op jit(solution)/shard_map/ppermute | solution.py:25
  22.5 0.9 %collective-permute-done.8.refs_2_ = bf16[64,64]{1,0:T(8,128)(2,1)S(1)} collective-permute-done((bf16[64,64]{1,0:T(8,128)(2,1)S(1)}, bf16[64,64]{1,0:T(8,128)(2,1)S(1)}, u32[]{:S(2)}, u32[]{:S(2)}) %collective-permute-start.8) | collective-permute-done | bytes 8224 | tf_op jit(solution)/shard_map/ppermute | solution.py:25
  23.4 0.0 collective-permute-done.6.refs_0_
  23.4 0.9 %finish.1 = bf16[64,1280]{1,0:T(8,128)(2,1)} custom-call(s32[1]{0:T(128)} %bitcast.col_ref, f32[64,1280]{1,0:T(8,128)S(1)} %begin.1.base, bf16[64,64]{1,0:T(8,128)(2,1)S(1)} %collective-permute-done.6.refs_0_, bf16[64,64]{1,0:T(8,128)(2,1)S(1)} %collective-permute-done.7.refs_1_, bf16[64,64]{1,0:T(8,128)(2,1)S(1)} %collective-permute-done.8.refs_2_, ...), custom_call_target="tpu_custom_call" | custom-call | tf_op jit(solution)/shard_map/finish/pallas_call | solution.py:267
  (2 shorter events, 0.0 us)
Async XLA Ops:
  0.6 7.4 %collective-permute-start.1 = (bf16[64,1280]{1,0:T(8,128)(2,1)}, bf16[64,1280]{1,0:T(8,128)(2,1)S(1)}, u32[]{:S(2)}, u32[]{:S(2)}) collective-permute-start(bf16[64,1280]{1,0:T(8,128)(2,1)} %bitcast.9), channel_id=1, source_target_pairs={{0,2},{1,3},{2,0},{3,1},{4,6},{5,7},{6,4},{7,5},{8,10},{9,11},{10,... | collective-permute-start | bytes 491528 | tf_op jit(solution)/shard_map/ppermute | solution.py:25
  3.7 11.6 %collective-permute-start = (bf16[64,1280]{1,0:T(8,128)(2,1)}, bf16[64,1280]{1,0:T(8,128)(2,1)S(1)}, u32[]{:S(2)}, u32[]{:S(2)}) collective-permute-start(bf16[64,1280]{1,0:T(8,128)(2,1)} %bitcast.10), channel_id=1, source_target_pairs={{0,1},{1,0},{2,3},{3,2},{4,5},{5,4},{6,7},{7,6},{8,9},{9,8},{10,11... | collective-permute-start | bytes 491528 | tf_op jit(solution)/shard_map/ppermute | solution.py:25
  8.1 7.8 %collective-permute-start.2 = (bf16[64,1280]{1,0:T(8,128)(2,1)S(1)}, bf16[64,1280]{1,0:T(8,128)(2,1)S(1)}, u32[]{:S(2)}, u32[]{:S(2)}) collective-permute-start(bf16[64,1280]{1,0:T(8,128)(2,1)S(1)} %collective-permute-done.1.refs_0_), channel_id=1, source_target_pairs={{0,1},{1,0},{2,3},{3,2},{4,5},{5,4},{6,7},{7,6},{8,9},{9,8},{10,11... | collective-permute-start | bytes 491528 | tf_op jit(solution)/shard_map/ppermute | solution.py:25
  8.1 8.3 %collective-permute-start.3 = (bf16[256,128]{1,0:T(8,128)(2,1)}, bf16[256,128]{1,0:T(8,128)(2,1)S(1)}, u32[]{:S(2)}, u32[]{:S(2)}) collective-permute-start(bf16[256,128]{1,0:T(8,128)(2,1)} %bitcast.13), channel_id=1, source_target_pairs={{0,4},{4,8},{8,12},{12,0},{1,5},{5,9},{9,13},{13,1},{2,6},{6,10},{... | collective-permute-start | bytes 196616 | tf_op jit(solution)/shard_map/ppermute | solution.py:40
  9.9 7.9 %collective-permute-start.4 = (bf16[256,128]{1,0:T(8,128)(2,1)}, bf16[256,128]{1,0:T(8,128)(2,1)S(1)}, u32[]{:S(2)}, u32[]{:S(2)}) collective-permute-start(bf16[256,128]{1,0:T(8,128)(2,1)} %bitcast.14), channel_id=1, source_target_pairs={{0,8},{4,12},{8,0},{12,4},{1,9},{5,13},{9,1},{13,5},{2,10},{6,14},... | collective-permute-start | bytes 196616 | tf_op jit(solution)/shard_map/ppermute | solution.py:40
  12.5 5.6 %collective-permute-start.5 = (bf16[256,128]{1,0:T(8,128)(2,1)}, bf16[256,128]{1,0:T(8,128)(2,1)S(1)}, u32[]{:S(2)}, u32[]{:S(2)}) collective-permute-start(bf16[256,128]{1,0:T(8,128)(2,1)} %bitcast.15), channel_id=1, source_target_pairs={{0,12},{4,0},{8,4},{12,8},{1,13},{5,1},{9,5},{13,9},{2,14},{6,2},{... | collective-permute-start | bytes 196616 | tf_op jit(solution)/shard_map/ppermute | solution.py:40
  18.7 3.8 %collective-permute-start.7 = (bf16[64,64]{1,0:T(8,128)(2,1)S(1)}, bf16[64,64]{1,0:T(8,128)(2,1)S(1)}, u32[]{:S(2)}, u32[]{:S(2)}) collective-permute-start(bf16[64,64]{1,0:T(8,128)(2,1)S(1)} %get-tuple-element.31), channel_id=1, source_target_pairs={{0,2},{1,3},{2,0},{3,1},{4,6},{5,7},{6,4},{7,5},{8,10},{9,11},{10,... | collective-permute-start | bytes 24584 | tf_op jit(solution)/shard_map/ppermute | solution.py:25
  20.2 3.2 %collective-permute-start.8 = (bf16[64,64]{1,0:T(8,128)(2,1)S(1)}, bf16[64,64]{1,0:T(8,128)(2,1)S(1)}, u32[]{:S(2)}, u32[]{:S(2)}) collective-permute-start(bf16[64,64]{1,0:T(8,128)(2,1)S(1)} %get-tuple-element.30), channel_id=1, source_target_pairs={{0,3},{1,2},{2,1},{3,0},{4,7},{5,6},{6,5},{7,4},{8,11},{9,10},{10,... | collective-permute-start | bytes 24584 | tf_op jit(solution)/shard_map/ppermute | solution.py:25
  20.9 2.5 %collective-permute-start.6 = (bf16[64,64]{1,0:T(8,128)(2,1)S(1)}, bf16[64,64]{1,0:T(8,128)(2,1)S(1)}, u32[]{:S(2)}, u32[]{:S(2)}) collective-permute-start(bf16[64,64]{1,0:T(8,128)(2,1)S(1)} %slice.9), channel_id=1, source_target_pairs={{0,1},{1,0},{2,3},{3,2},{4,5},{5,4},{6,7},{7,6},{8,9},{9,8},{10,11... | collective-permute-start | bytes 24584 | tf_op jit(solution)/shard_map/ppermute | solution.py:25

commit v2 on v1

--- a/solution.py
+++ b/solution.py
@@ -33,11 +33,17 @@
     return sorted(plan, key=lambda step: (bin(step[0]).count("1"), -step[2]))
 
 
+def folded_ring(size):
+    return [0, *range(1, size, 2), *reversed(range(2, size, 2))]
+
+
 def gather_bands(block, axis):
     size = lax.axis_size(axis)
+    ring = folded_ring(size)
     blocks = []
     for step in range(1, size):
-        blocks.append(lax.ppermute(block, axis, [(i, (i + step) % size) for i in range(size)]))
+        pairs = [(ring[i], ring[(i + step) % size]) for i in range(size)]
+        blocks.append(lax.ppermute(block, axis, pairs))
     return blocks
 
 
@@ -221,41 +227,38 @@
     return w_ref[pl.ds(pl.multiple_of(head * head_size, head_size), head_size), :]
 
 
-def begin_kernel(col_ref, home, w_ref, bias, hidden, out_ref):
-    own = home[: hidden.shape[0], :]
-    product = jnp.dot(
-        own, head_rows(col_ref, 0, w_ref, own.shape[1]), preferred_element_type=jnp.float32
-    )
-    out_ref[...] = product + bias[...].reshape(1, -1) + hidden[...].astype(jnp.float32)
-
-
-def begin(col, home, w_out, bias, hidden):
-    return pl.pallas_call(
-        begin_kernel,
+def begin_kernel(masks, col_ref, home, *refs):
+    *parts, w_ref, bias, hidden, out_ref = refs
+    head_size = home.shape[1]
+    total = bias[...].reshape(1, -1) + hidden[...].astype(jnp.float32)
+    for mask, part in zip((0, *masks), (home[: hidden.shape[0], :], *(p[...] for p in parts))):
+        total = total + jnp.dot(
+            part, head_rows(col_ref, mask, w_ref, head_size), preferred_element_type=jnp.float32
+        )
+    out_ref[...] = total
+
+
+def begin(col, home, parts, w_out, bias, hidden):
+    return pl.pallas_call(
+        functools.partial(begin_kernel, tuple(parts)),
         out_shape=pltpu.VMEM(hidden.shape, jnp.float32),
-        in_specs=[SMEM] + [VMEM] * 4,
+        in_specs=[SMEM] + [VMEM] * (4 + len(parts)),
         out_specs=VMEM,
         compiler_params=PARAMS,
         name="begin",
-    )(col, *near(home, w_out, bias, hidden))
-
-
-def finish_kernel(col_ref, base, *refs):
-    *parts, w_ref, out_ref, ready, sent = refs
-    head_size = parts[0].shape[1]
-    rows = [head_rows(col_ref, mask, w_ref, head_size) for mask in range(1, len(parts) + 1)]
-    values = [part[...] for part in parts]
+    )(col, *near(home, *parts.values(), w_out, bias, hidden))
+
+
+def finish_kernel(mask, col_ref, base, part, w_ref, out_ref, ready, sent):
+    rows = head_rows(col_ref, mask, w_ref, part.shape[1])
+    values = part[...]
     channels = base.shape[1]
     step = channels // 2 if channels % 256 == 0 else channels
     copies = []
     for index, start in enumerate(range(0, channels, step)):
         columns = slice(start, start + step)
-        total = base[:, columns]
-        for value, row in zip(values, rows):
-            total = total + jnp.dot(
-                value, row[:, columns], preferred_element_type=jnp.float32
-            )
-        ready[:, columns] = total.astype(jnp.bfloat16)
+        product = jnp.dot(values, rows[:, columns], preferred_element_type=jnp.float32)
+        ready[:, columns] = (base[:, columns] + product).astype(jnp.bfloat16)
         copy = pltpu.make_async_copy(ready.at[:, columns], out_ref.at[:, columns], sent.at[index])
         copy.start()
         copies.append(copy)
@@ -263,16 +266,16 @@
         copy.wait()
 
 
-def finish(col, base, parts, w_out):
-    return pl.pallas_call(
-        finish_kernel,
+def finish(col, base, mask, part, w_out):
+    return pl.pallas_call(
+        functools.partial(finish_kernel, mask),
         out_shape=jax.ShapeDtypeStruct(base.shape, jnp.bfloat16),
-        in_specs=[SMEM] + [VMEM] * (len(parts) + 2),
+        in_specs=[SMEM] + [VMEM] * 3,
         out_specs=HBM,
         scratch_shapes=[pltpu.VMEM(base.shape, jnp.bfloat16), pltpu.SemaphoreType.DMA((2,))],
         compiler_params=PARAMS,
         name="finish",
-    )(col, *near(base, *parts, w_out))
+    )(col, *near(base, part, w_out))
 
 
 def shards(hidden, ln_gain, ln_bias, w_query, w_keyval, stale_keyval, w_out, out_bias):
@@ -299,8 +302,9 @@
         block = away if mask >= half else home
         at = (mask % half) * each
         mine[mask] = swap(block[at : at + each], "cols", mask)
-    base = begin(col, home, near_out, near_bias, near_own)
-    output = finish(col, base, [mine[m] for m in range(1, size)], near_out)
+    last = mine.pop(half)
+    base = begin(col, home, mine, near_out, near_bias, near_own)
+    output = finish(col, base, half, last, near_out)
     return (
         output.reshape(hidden.shape),
         fresh.reshape(band_rows, size * strip_cols, 1, 2 * head_size),

time: 24.5 us -> 25.5 us (1.041)
  waiting for transfers between devices: 7.62 us -> 8.52 us
    ppermute x6, waiting for transfers between devices: 6 us -> 7.33 us  [swap(): return lax.ppermute(block, axis, [(i, i ^ mask) for i in range(size)])]
    ppermute x3, waiting for transfers between devices: 1.61 us -> 1.19 us  [gather_bands(): blocks.append(lax.ppermute(block, axis, pairs))]
where the time goes in v2:
time: 25.5 us; the launch traced here: 25.3 us
  starting transfers between devices  11.2 us (44%)
  waiting for transfers between devices  8.52 us (33%)
  Pallas kernels  4.92 us (19%)
  between operations  0.72 us (3%)
    ppermute x6, waiting for transfers between devices, swap(): return lax.ppermute(block, axis, [(i, i ^ mask) for i in range(size)])  7.33 us
    ppermute x3, starting transfers between devices, gather_bands(): blocks.append(lax.ppermute(block, axis, pairs))  5.88 us
    ppermute x6, starting transfers between devices, swap(): return lax.ppermute(block, axis, [(i, i ^ mask) for i in range(size)])  5.31 us
    pallas_call x1, Pallas kernels, load(): pl.pallas_call(functools.partial(load_kernel, count), out_shape=tuple((pl...  1.41 us
    ppermute x3, waiting for transfers between devices, gather_bands(): blocks.append(lax.ppermute(block, axis, pairs))  1.19 us
    pallas_call x2, Pallas kernels, project(): pl.pallas_call(functools.partial(project_kernel, len(strips)), out_shape=...  1.13 us
    pallas_call x1, Pallas kernels, finish(): pl.pallas_call(functools.partial(finish_kernel, mask), out_shape=jax.Shap...  0.84 us
    pallas_call x1, Pallas kernels, attend_home(): pl.pallas_call(functools.partial(home_kernel, len(keys), head_size, tile)...  0.65 us
  transfers between devices with their start and end apart: 9, of which 5 were waited for; matrix products, arithmetic and copies ran while one was open for 0% of the time, Pallas kernels for 14%

profile of v2, /device:TPU:0, one launch (start us, length us, event | category | flops | bytes accessed | tf_op | source)
XLA Modules:
  0.0 25.3 jit_solution(13445027334298601089)
XLA Ops:
  0.6 3.0 %collective-permute-start.1 = (bf16[64,1280]{1,0:T(8,128)(2,1)}, bf16[64,1280]{1,0:T(8,128)(2,1)S(1)}, u32[]{:S(2)}, u32[]{:S(2)}) collective-permute-start(bf16[64,1280]{1,0:T(8,128)(2,1)} %bitcast.9), channel_id=1, source_target_pairs={{0,2},{1,3},{2,0},{3,1},{4,6},{5,7},{6,4},{7,5},{8,10},{9,11},{10,... | collective-permute-start | bytes 491528 | tf_op jit(solution)/shard_map/ppermute | solution.py:25
  3.7 0.0 collective-permute-start
  3.7 4.4 %collective-permute-done.1.refs_0_ = bf16[64,1280]{1,0:T(8,128)(2,1)S(1)} collective-permute-done((bf16[64,1280]{1,0:T(8,128)(2,1)}, bf16[64,1280]{1,0:T(8,128)(2,1)S(1)}, u32[]{:S(2)}, u32[]{:S(2)}) %collective-permute-start.1) | collective-permute-done | bytes 163872 | tf_op jit(solution)/shard_map/ppermute | solution.py:25
  8.1 0.0 collective-permute-start.2
  8.1 1.8 %collective-permute-start.3 = (bf16[256,128]{1,0:T(8,128)(2,1)}, bf16[256,128]{1,0:T(8,128)(2,1)S(1)}, u32[]{:S(2)}, u32[]{:S(2)}) collective-permute-start(bf16[256,128]{1,0:T(8,128)(2,1)} %bitcast.13), channel_id=1, source_target_pairs={{0,4},{4,12},{12,8},{8,0},{1,5},{5,13},{13,9},{9,1},{2,6},{6,14},{... | collective-permute-start | bytes 196616 | tf_op jit(solution)/shard_map/ppermute | solution.py:46
  9.9 2.5 %collective-permute-start.4 = (bf16[256,128]{1,0:T(8,128)(2,1)}, bf16[256,128]{1,0:T(8,128)(2,1)S(1)}, u32[]{:S(2)}, u32[]{:S(2)}) collective-permute-start(bf16[256,128]{1,0:T(8,128)(2,1)} %bitcast.14), channel_id=1, source_target_pairs={{0,12},{4,8},{12,0},{8,4},{1,13},{5,9},{13,1},{9,5},{2,14},{6,10},... | collective-permute-start | bytes 196616 | tf_op jit(solution)/shard_map/ppermute | solution.py:46
  12.4 1.6 %collective-permute-start.5 = (bf16[256,128]{1,0:T(8,128)(2,1)}, bf16[256,128]{1,0:T(8,128)(2,1)S(1)}, u32[]{:S(2)}, u32[]{:S(2)}) collective-permute-start(bf16[256,128]{1,0:T(8,128)(2,1)} %bitcast.15), channel_id=1, source_target_pairs={{0,8},{4,0},{12,4},{8,12},{1,9},{5,1},{13,5},{9,13},{2,10},{6,2},{... | collective-permute-start | bytes 196616 | tf_op jit(solution)/shard_map/ppermute | solution.py:46
  14.0 1.4 %load.1 = (bf16[64,1280]{1,0:T(8,128)(2,1)S(1)}, bf16[256,1280]{1,0:T(8,128)(2,1)S(1)}, f32[1280]{0:T(1024)S(1)}, f32[1280]{0:T(1024)S(1)}, f32[1280]{0:T(1024)S...) custom-call(bf16[64,1280]{1,0:T(8,128)(2,1)} %bitcast.11, bf16[256,1280]{1,0:T(8,128)(2,1)} %refs_1_.1, ...), custom_call_target="tpu_custom_call" | custom-call | tf_op jit(solution)/shard_map/load/pallas_call | solution.py:92
  15.4 0.0 collective-permute-done.refs_1_
  15.4 0.6 %project.2 = (bf16[128,128]{1,0:T(8,128)(2,1)S(1)}, bf16[128,128]{1,0:T(8,128)(2,1)S(1)}) custom-call(bf16[64,1280]{1,0:T(8,128)(2,1)S(1)} %get-tuple-element.15.refs_0_.refs_4_, bf16[64,1280]{1,0:T(8,128)(2,1)S(1)} %collective-permute-done.refs_1_, f32[1280]{0:T(1024)S(1)} %get-tuple-element.16.refs_2_, f32[1280]{0:T(1024)S(1)} %get-tuple-element.17.refs_3_, ...), custom_call_target="tpu_custom_call" | custom-call | tf_op jit(solution)/shard_map/project/pallas_call | solution.py:110
  16.0 0.0 collective-permute-done.2.refs_1_
  16.0 0.6 %project.3 = (bf16[128,128]{1,0:T(8,128)(2,1)S(1)}, bf16[128,128]{1,0:T(8,128)(2,1)S(1)}) custom-call(bf16[64,1280]{1,0:T(8,128)(2,1)S(1)} %collective-permute-done.1.refs_0_, bf16[64,1280]{1,0:T(8,128)(2,1)S(1)} %collective-permute-done.2.refs_1_, f32[1280]{0:T(1024)S(1)} %get-tuple-element.16.refs_2_, f32[1280]{0:T(1024)S(1)} %get-tuple-element.17.refs_3_, ...), custom_call_target="tpu_custom_call" | custom-call | tf_op jit(solution)/shard_map/project/pallas_call | solution.py:110
  16.5 0.0 collective-permute-done.3.refs_2_
  16.6 0.4 %collective-permute-done.4.refs_3_ = bf16[256,128]{1,0:T(8,128)(2,1)S(1)} collective-permute-done((bf16[256,128]{1,0:T(8,128)(2,1)}, bf16[256,128]{1,0:T(8,128)(2,1)S(1)}, u32[]{:S(2)}, u32[]{:S(2)}) %collective-permute-start.4) | collective-permute-done | bytes 65568 | tf_op jit(solution)/shard_map/ppermute | solution.py:46
  17.0 0.8 %collective-permute-done.5.refs_4_ = bf16[256,128]{1,0:T(8,128)(2,1)S(1)} collective-permute-done((bf16[256,128]{1,0:T(8,128)(2,1)}, bf16[256,128]{1,0:T(8,128)(2,1)S(1)}, u32[]{:S(2)}, u32[]{:S(2)}) %collective-permute-start.5) | collective-permute-done | bytes 65568 | tf_op jit(solution)/shard_map/ppermute | solution.py:46
  17.7 0.6 %attend_away.1 = bf16[128,64]{1,0:T(8,128)(2,1)S(1)} custom-call(bf16[128,128]{1,0:T(8,128)(2,1)S(1)} %get-tuple-element.24.q_ref, bf16[128,128]{1,0:T(8,128)(2,1)S(1)} %get-tuple-element.21.refs_0_, bf16[128,128]{1,0:T(8,128)(2,1)S(1)} %get-tuple-element.22.refs_1_, bf16[256,128]{1,0:T(8,128)(2,1)S(1)} %collective-permute-done.3.refs_2_, ...), custom_call_target="tpu_custom_call" | custom-call | tf_op jit(solution)/shard_map/attend_away/pallas_call | solution.py:175
  18.4 1.0 %collective-permute-start.6 = (bf16[64,64]{1,0:T(8,128)(2,1)S(1)}, bf16[64,64]{1,0:T(8,128)(2,1)S(1)}, u32[]{:S(2)}, u32[]{:S(2)}) collective-permute-start(bf16[64,64]{1,0:T(8,128)(2,1)S(1)} %get-tuple-element.31), channel_id=1, source_target_pairs={{0,3},{1,2},{2,1},{3,0},{4,7},{5,6},{6,5},{7,4},{8,11},{9,10},{10,... | collective-permute-start | bytes 24584 | tf_op jit(solution)/shard_map/ppermute | solution.py:25
  19.4 0.6 %attend_home.1 = (bf16[128,64]{1,0:T(8,128)(2,1)S(1)}, bf16[8,4,8,128]{3,2,1,0:T(8,128)(2,1)}) custom-call(s32[1]{0:T(128)} %bitcast.col_ref, bf16[128,128]{1,0:T(8,128)(2,1)S(1)} %get-tuple-element.20.q_ref, bf16[128,128]{1,0:T(8,128)(2,1)S(1)} %get-tuple-element.21.refs_0_, bf16[128,128]{1,0:T(8,128)(2,1)S(1)} %get-tuple-element.22.refs_1_, ...), custom_call_target="tpu_custom_call" | custom-call | tf_op jit(solution)/shard_map/attend_home/pallas_call | solution.py:207
  20.1 0.7 %collective-permute-start.7 = (bf16[64,64]{1,0:T(8,128)(2,1)S(1)}, bf16[64,64]{1,0:T(8,128)(2,1)S(1)}, u32[]{:S(2)}, u32[]{:S(2)}) collective-permute-start(bf16[64,64]{1,0:T(8,128)(2,1)S(1)} %slice.10), channel_id=1, source_target_pairs={{0,1},{1,0},{2,3},{3,2},{4,5},{5,4},{6,7},{7,6},{8,9},{9,8},{10,11... | collective-permute-start | bytes 24584 | tf_op jit(solution)/shard_map/ppermute | solution.py:25
  20.8 0.5 %collective-permute-start.8 = (bf16[64,64]{1,0:T(8,128)(2,1)S(1)}, bf16[64,64]{1,0:T(8,128)(2,1)S(1)}, u32[]{:S(2)}, u32[]{:S(2)}) collective-permute-start(bf16[64,64]{1,0:T(8,128)(2,1)S(1)} %get-tuple-element.30), channel_id=1, source_target_pairs={{0,2},{1,3},{2,0},{3,1},{4,6},{5,7},{6,4},{7,5},{8,10},{9,11},{10,... | collective-permute-start | bytes 24584 | tf_op jit(solution)/shard_map/ppermute | solution.py:25
  21.3 0.4 %collective-permute-done.6.refs_0_ = bf16[64,64]{1,0:T(8,128)(2,1)S(1)} collective-permute-done((bf16[64,64]{1,0:T(8,128)(2,1)S(1)}, bf16[64,64]{1,0:T(8,128)(2,1)S(1)}, u32[]{:S(2)}, u32[]{:S(2)}) %collective-permute-start.6) | collective-permute-done | bytes 8224 | tf_op jit(solution)/shard_map/ppermute | solution.py:25
  21.7 0.0 collective-permute-done.7.refs_1_
  21.7 0.3 %begin.1.base = f32[64,1280]{1,0:T(8,128)S(1)} custom-call(s32[1]{0:T(128)} %bitcast.col_ref, bf16[128,64]{1,0:T(8,128)(2,1)S(1)} %get-tuple-element.23.home, bf16[64,64]{1,0:T(8,128)(2,1)S(1)} %collective-permute-done.6.refs_0_, bf16[64,64]{1,0:T(8,128)(2,1)S(1)} %collective-permute-done.7.refs_1_, bf16[256,1280]{1,0:T(8,128)(2,1)S(1)} %get-tuple-element.25.refs_2_.w_ref, ...), custom_call_target="tpu_custom_call" | custom-call | tf_op jit(solution)/shard_map/begin/pallas_call | solution.py:242
  22.0 2.5 %collective-permute-done.8.part = bf16[64,64]{1,0:T(8,128)(2,1)S(1)} collective-permute-done((bf16[64,64]{1,0:T(8,128)(2,1)S(1)}, bf16[64,64]{1,0:T(8,128)(2,1)S(1)}, u32[]{:S(2)}, u32[]{:S(2)}) %collective-permute-start.8) | collective-permute-done | bytes 8224 | tf_op jit(solution)/shard_map/ppermute | solution.py:25
  24.5 0.8 %finish.1 = bf16[64,1280]{1,0:T(8,128)(2,1)} custom-call(s32[1]{0:T(128)} %bitcast.col_ref, f32[64,1280]{1,0:T(8,128)S(1)} %begin.1.base, bf16[64,64]{1,0:T(8,128)(2,1)S(1)} %collective-permute-done.8.part, bf16[256,1280]{1,0:T(8,128)(2,1)S(1)} %get-tuple-element.25.refs_2_.w_ref), custom_call_target="tpu_custom_call" | custom-call | tf_op jit(solution)/shard_map/finish/pallas_call | solution.py:270
  (2 shorter events, 0.0 us)
Async XLA Ops:
  0.6 7.4 %collective-permute-start.1 = (bf16[64,1280]{1,0:T(8,128)(2,1)}, bf16[64,1280]{1,0:T(8,128)(2,1)S(1)}, u32[]{:S(2)}, u32[]{:S(2)}) collective-permute-start(bf16[64,1280]{1,0:T(8,128)(2,1)} %bitcast.9), channel_id=1, source_target_pairs={{0,2},{1,3},{2,0},{3,1},{4,6},{5,7},{6,4},{7,5},{8,10},{9,11},{10,... | collective-permute-start | bytes 491528 | tf_op jit(solution)/shard_map/ppermute | solution.py:25
  3.7 11.7 %collective-permute-start = (bf16[64,1280]{1,0:T(8,128)(2,1)}, bf16[64,1280]{1,0:T(8,128)(2,1)S(1)}, u32[]{:S(2)}, u32[]{:S(2)}) collective-permute-start(bf16[64,1280]{1,0:T(8,128)(2,1)} %bitcast.10), channel_id=1, source_target_pairs={{0,1},{1,0},{2,3},{3,2},{4,5},{5,4},{6,7},{7,6},{8,9},{9,8},{10,11... | collective-permute-start | bytes 491528 | tf_op jit(solution)/shard_map/ppermute | solution.py:25
  8.1 7.9 %collective-permute-start.2 = (bf16[64,1280]{1,0:T(8,128)(2,1)S(1)}, bf16[64,1280]{1,0:T(8,128)(2,1)S(1)}, u32[]{:S(2)}, u32[]{:S(2)}) collective-permute-start(bf16[64,1280]{1,0:T(8,128)(2,1)S(1)} %collective-permute-done.1.refs_0_), channel_id=1, source_target_pairs={{0,1},{1,0},{2,3},{3,2},{4,5},{5,4},{6,7},{7,6},{8,9},{9,8},{10,11... | collective-permute-start | bytes 491528 | tf_op jit(solution)/shard_map/ppermute | solution.py:25
  8.1 8.5 %collective-permute-start.3 = (bf16[256,128]{1,0:T(8,128)(2,1)}, bf16[256,128]{1,0:T(8,128)(2,1)S(1)}, u32[]{:S(2)}, u32[]{:S(2)}) collective-permute-start(bf16[256,128]{1,0:T(8,128)(2,1)} %bitcast.13), channel_id=1, source_target_pairs={{0,4},{4,12},{12,8},{8,0},{1,5},{5,13},{13,9},{9,1},{2,6},{6,14},{... | collective-permute-start | bytes 196616 | tf_op jit(solution)/shard_map/ppermute | solution.py:46
  9.9 7.1 %collective-permute-start.4 = (bf16[256,128]{1,0:T(8,128)(2,1)}, bf16[256,128]{1,0:T(8,128)(2,1)S(1)}, u32[]{:S(2)}, u32[]{:S(2)}) collective-permute-start(bf16[256,128]{1,0:T(8,128)(2,1)} %bitcast.14), channel_id=1, source_target_pairs={{0,12},{4,8},{12,0},{8,4},{1,13},{5,9},{13,1},{9,5},{2,14},{6,10},... | collective-permute-start | bytes 196616 | tf_op jit(solution)/shard_map/ppermute | solution.py:46
  12.4 5.4 %collective-permute-start.5 = (bf16[256,128]{1,0:T(8,128)(2,1)}, bf16[256,128]{1,0:T(8,128)(2,1)S(1)}, u32[]{:S(2)}, u32[]{:S(2)}) collective-permute-start(bf16[256,128]{1,0:T(8,128)(2,1)} %bitcast.15), channel_id=1, source_target_pairs={{0,8},{4,0},{12,4},{8,12},{1,9},{5,1},{13,5},{9,13},{2,10},{6,2},{... | collective-permute-start | bytes 196616 | tf_op jit(solution)/shard_map/ppermute | solution.py:46
  18.4 3.4 %collective-permute-start.6 = (bf16[64,64]{1,0:T(8,128)(2,1)S(1)}, bf16[64,64]{1,0:T(8,128)(2,1)S(1)}, u32[]{:S(2)}, u32[]{:S(2)}) collective-permute-start(bf16[64,64]{1,0:T(8,128)(2,1)S(1)} %get-tuple-element.31), channel_id=1, source_target_pairs={{0,3},{1,2},{2,1},{3,0},{4,7},{5,6},{6,5},{7,4},{8,11},{9,10},{10,... | collective-permute-start | bytes 24584 | tf_op jit(solution)/shard_map/ppermute | solution.py:25
  20.1 1.7 %collective-permute-start.7 = (bf16[64,64]{1,0:T(8,128)(2,1)S(1)}, bf16[64,64]{1,0:T(8,128)(2,1)S(1)}, u32[]{:S(2)}, u32[]{:S(2)}) collective-permute-start(bf16[64,64]{1,0:T(8,128)(2,1)S(1)} %slice.10), channel_id=1, source_target_pairs={{0,1},{1,0},{2,3},{3,2},{4,5},{5,4},{6,7},{7,6},{8,9},{9,8},{10,11... | collective-permute-start | bytes 24584 | tf_op jit(solution)/shard_map/ppermute | solution.py:25
  20.8 3.7 %collective-permute-start.8 = (bf16[64,64]{1,0:T(8,128)(2,1)S(1)}, bf16[64,64]{1,0:T(8,128)(2,1)S(1)}, u32[]{:S(2)}, u32[]{:S(2)}) collective-permute-start(bf16[64,64]{1,0:T(8,128)(2,1)S(1)} %get-tuple-element.30), channel_id=1, source_target_pairs={{0,2},{1,3},{2,0},{3,1},{4,6},{5,7},{6,4},{7,5},{8,10},{9,11},{10,... | collective-permute-start | bytes 24584 | tf_op jit(solution)/shard_map/ppermute | solution.py:25

commit v3 on v2

--- a/solution.py
+++ b/solution.py
@@ -53,26 +53,6 @@
     for mask, source, bit in gather_plan(size):
         blocks[mask] = swap(blocks[source], axis, bit)
     return [blocks[m] for m in range(size)]
-
-
-def project_rows(strips, gain, bias, w_query, w_keyval, q_out, kv_out):
-    scale, shift = gain[...].reshape(1, -1), bias[...].reshape(1, -1)
-    normed = []
-    for strip in strips:
-        values = strip[...].astype(jnp.float32)
-        centred = values - jnp.mean(values, axis=-1, keepdims=True)
-        variance = jnp.mean(centred * centred, axis=-1, keepdims=True)
-        normed.append(
-            (centred * lax.rsqrt(variance + 1e-05) * scale + shift).astype(jnp.bfloat16)
-        )
-    both = jnp.concatenate(normed, axis=0)
-    queries = lax.dot_general(
-        both, w_query[...], (((1,), (1,)), ((), ())), preferred_element_type=jnp.float32
-    ).astype(jnp.bfloat16)
-    q_out[...] = jnp.concatenate([queries, jnp.zeros_like(queries)], axis=1)
-    kv_out[...] = jnp.dot(both, w_keyval[...], preferred_element_type=jnp.float32).astype(
-        jnp.bfloat16
-    )
 
 
 def load_kernel(count, *refs):
@@ -101,17 +81,36 @@
 
 
 def project_kernel(count, *refs):
-    project_rows(refs[:count], *refs[count:])
-
-
-def project(strips, *params):
-    rows = len(strips) * strips[0].shape[0]
+    strips, (gain, bias, w_query, w_keyval), outs = refs[:count], refs[count : count + 4], refs[count + 4 :]
+    scale, shift = gain[...].reshape(1, -1), bias[...].reshape(1, -1)
+    normed = []
+    for strip in strips:
+        values = strip[...].astype(jnp.float32)
+        centred = values - jnp.mean(values, axis=-1, keepdims=True)
+        variance = jnp.mean(centred * centred, axis=-1, keepdims=True)
+        normed.append(
+            (centred * lax.rsqrt(variance + 1e-05) * scale + shift).astype(jnp.bfloat16)
+        )
+    rows = jnp.concatenate(normed, axis=0)
+    queries = lax.dot_general(
+        rows, w_query[...], (((1,), (1,)), ((), ())), preferred_element_type=jnp.float32
+    ).astype(jnp.bfloat16)
+    keyval = jnp.dot(rows, w_keyval[...], preferred_element_type=jnp.float32).astype(jnp.bfloat16)
+    middle = outs[0].shape[0]
+    for index, part in enumerate((slice(0, middle), slice(middle, None))):
+        chosen = queries[part]
+        outs[2 * index][...] = jnp.concatenate([chosen, jnp.zeros_like(chosen)], axis=1)
+        outs[2 * index + 1][...] = keyval[part]
+
+
+def project(strips, params):
+    rows = len(strips) // 2 * strips[0].shape[0]
     shape = pltpu.VMEM((rows, params[-1].shape[1]), jnp.bfloat16)
     return pl.pallas_call(
         functools.partial(project_kernel, len(strips)),
-        out_shape=(shape, shape),
+        out_shape=(shape,) * 4,
         in_specs=[VMEM] * (len(strips) + len(params)),
-        out_specs=(VMEM, VMEM),
+        out_specs=(VMEM,) * 4,
         compiler_params=PARAMS,
         name="project",
     )(*near(*strips, *params))
@@ -291,8 +290,7 @@
     near_own, near_out, near_bias, *params = load(
         own, w_out, out_bias, ln_gain, ln_bias, w_query.T, w_keyval
     )
-    q_home, kv_home = project([near_own, *strips[1:half]], *params)
-    q_away, kv_away = project(strips[half:], *params)
+    q_home, kv_home, q_away, kv_away = project([near_own, *strips[1:]], params)
     keys = [kv_home, kv_away] + stale
     away = attend_away(q_away, keys, head_size)
     fresh_shape = (band_rows, size, strip_cols, 2 * head_size)

time: 25.5 us -> 25.5 us (level)
  waiting for transfers between devices: 8.52 us -> 8.83 us
  Pallas kernels: 4.92 us -> 4.62 us
    ppermute x3, waiting for transfers between devices: 1.19 us -> 1.49 us  [gather_bands(): blocks.append(lax.ppermute(block, axis, pairs))]
    pallas_call x2 -> x1, Pallas kernels: 1.13 us -> 0.83 us  [project(): pl.pallas_call(functools.partial(project_kernel, len(strips)), out_shape=...]
  transfers between devices with their start and end apart: 9 -> 9, of which waited for: 5 -> 5; matrix products, arithmetic and copies ran while one was open for 0% -> 0% of each run, Pallas kernels for 14% -> 12%
where the time goes in v3:
time: 25.5 us; the launch traced here: 25.4 us
  starting transfers between devices  11.2 us (44%)
  waiting for transfers between devices  8.83 us (35%)
  Pallas kernels  4.62 us (18%)
  between operations  0.71 us (3%)
    ppermute x6, waiting for transfers between devices, swap(): return lax.ppermute(block, axis, [(i, i ^ mask) for i in range(size)])  7.34 us
    ppermute x3, starting transfers between devices, gather_bands(): blocks.append(lax.ppermute(block, axis, pairs))  5.88 us
    ppermute x6, starting transfers between devices, swap(): return lax.ppermute(block, axis, [(i, i ^ mask) for i in range(size)])  5.31 us
    ppermute x3, waiting for transfers between devices, gather_bands(): blocks.append(lax.ppermute(block, axis, pairs))  1.49 us
    pallas_call x1, Pallas kernels, load(): pl.pallas_call(functools.partial(load_kernel, count), out_shape=tuple((pl...  1.41 us
    pallas_call x1, Pallas kernels, finish(): pl.pallas_call(functools.partial(finish_kernel, mask), out_shape=jax.Shap...  0.84 us
    pallas_call x1, Pallas kernels, project(): pl.pallas_call(functools.partial(project_kernel, len(strips)), out_shape=...  0.83 us
    pallas_call x1, Pallas kernels, attend_home(): pl.pallas_call(functools.partial(home_kernel, len(keys), head_size, tile)...  0.65 us
  transfers between devices with their start and end apart: 9, of which 5 were waited for; matrix products, arithmetic and copies ran while one was open for 0% of the time, Pallas kernels for 12%

profile of v3, /device:TPU:0, one launch (start us, length us, event | category | flops | bytes accessed | tf_op | source)
XLA Modules:
  0.0 25.4 jit_solution(13300781573047913223)
XLA Ops:
  0.6 3.0 %collective-permute-start.1 = (bf16[64,1280]{1,0:T(8,128)(2,1)}, bf16[64,1280]{1,0:T(8,128)(2,1)S(1)}, u32[]{:S(2)}, u32[]{:S(2)}) collective-permute-start(bf16[64,1280]{1,0:T(8,128)(2,1)} %bitcast.9), channel_id=1, source_target_pairs={{0,2},{1,3},{2,0},{3,1},{4,6},{5,7},{6,4},{7,5},{8,10},{9,11},{10,... | collective-permute-start | bytes 491528 | tf_op jit(solution)/shard_map/ppermute | solution.py:25
  3.7 0.0 collective-permute-start
  3.7 4.4 %collective-permute-done.1.refs_2_ = bf16[64,1280]{1,0:T(8,128)(2,1)S(1)} collective-permute-done((bf16[64,1280]{1,0:T(8,128)(2,1)}, bf16[64,1280]{1,0:T(8,128)(2,1)S(1)}, u32[]{:S(2)}, u32[]{:S(2)}) %collective-permute-start.1) | collective-permute-done | bytes 163872 | tf_op jit(solution)/shard_map/ppermute | solution.py:25
  8.1 0.0 collective-permute-start.2
  8.1 1.8 %collective-permute-start.3 = (bf16[256,128]{1,0:T(8,128)(2,1)}, bf16[256,128]{1,0:T(8,128)(2,1)S(1)}, u32[]{:S(2)}, u32[]{:S(2)}) collective-permute-start(bf16[256,128]{1,0:T(8,128)(2,1)} %bitcast.13), channel_id=1, source_target_pairs={{0,4},{4,12},{12,8},{8,0},{1,5},{5,13},{13,9},{9,1},{2,6},{6,14},{... | collective-permute-start | bytes 196616 | tf_op jit(solution)/shard_map/ppermute | solution.py:46
  9.9 2.5 %collective-permute-start.4 = (bf16[256,128]{1,0:T(8,128)(2,1)}, bf16[256,128]{1,0:T(8,128)(2,1)S(1)}, u32[]{:S(2)}, u32[]{:S(2)}) collective-permute-start(bf16[256,128]{1,0:T(8,128)(2,1)} %bitcast.14), channel_id=1, source_target_pairs={{0,12},{4,8},{12,0},{8,4},{1,13},{5,9},{13,1},{9,5},{2,14},{6,10},... | collective-permute-start | bytes 196616 | tf_op jit(solution)/shard_map/ppermute | solution.py:46
  12.4 1.6 %collective-permute-start.5 = (bf16[256,128]{1,0:T(8,128)(2,1)}, bf16[256,128]{1,0:T(8,128)(2,1)S(1)}, u32[]{:S(2)}, u32[]{:S(2)}) collective-permute-start(bf16[256,128]{1,0:T(8,128)(2,1)} %bitcast.15), channel_id=1, source_target_pairs={{0,8},{4,0},{12,4},{8,12},{1,9},{5,1},{13,5},{9,13},{2,10},{6,2},{... | collective-permute-start | bytes 196616 | tf_op jit(solution)/shard_map/ppermute | solution.py:46
  14.0 1.4 %load.1 = (bf16[64,1280]{1,0:T(8,128)(2,1)S(1)}, bf16[256,1280]{1,0:T(8,128)(2,1)S(1)}, f32[1280]{0:T(1024)S(1)}, f32[1280]{0:T(1024)S(1)}, f32[1280]{0:T(1024)S...) custom-call(bf16[64,1280]{1,0:T(8,128)(2,1)} %bitcast.11, bf16[256,1280]{1,0:T(8,128)(2,1)} %refs_1_.1, ...), custom_call_target="tpu_custom_call" | custom-call | tf_op jit(solution)/shard_map/load/pallas_call | solution.py:72
  15.4 0.0 collective-permute-done.refs_1_
  15.4 0.0 collective-permute-done.2.refs_3_
  15.4 0.8 %project.1 = (bf16[128,128]{1,0:T(8,128)(2,1)S(1)}, bf16[128,128]{1,0:T(8,128)(2,1)S(1)}, bf16[128,128]{1,0:T(8,128)(2,1)S(1)}, bf16[128,128]{1,0:T(8,128)(2,1)S(1)}) custom-call(bf16[64,1280]{1,0:T(8,128)(2,1)S(1)} %get-tuple-element.15.refs_0_.refs_4_, bf16[64,1280]{1,0:T(8,128)(2,1)S(1)} %collective-permute-done.refs_1_, ...), custom_call_target="tpu_custom_call" | custom-call | tf_op jit(solution)/shard_map/project/pallas_call | solution.py:109
  16.2 0.0 collective-permute-done.3.refs_2_
  16.2 0.7 %collective-permute-done.4.refs_3_ = bf16[256,128]{1,0:T(8,128)(2,1)S(1)} collective-permute-done((bf16[256,128]{1,0:T(8,128)(2,1)}, bf16[256,128]{1,0:T(8,128)(2,1)S(1)}, u32[]{:S(2)}, u32[]{:S(2)}) %collective-permute-start.4) | collective-permute-done | bytes 65568 | tf_op jit(solution)/shard_map/ppermute | solution.py:46
  17.0 0.8 %collective-permute-done.5.refs_4_ = bf16[256,128]{1,0:T(8,128)(2,1)S(1)} collective-permute-done((bf16[256,128]{1,0:T(8,128)(2,1)}, bf16[256,128]{1,0:T(8,128)(2,1)S(1)}, u32[]{:S(2)}, u32[]{:S(2)}) %collective-permute-start.5) | collective-permute-done | bytes 65568 | tf_op jit(solution)/shard_map/ppermute | solution.py:46
  17.7 0.6 %attend_away.1 = bf16[128,64]{1,0:T(8,128)(2,1)S(1)} custom-call(bf16[128,128]{1,0:T(8,128)(2,1)S(1)} %get-tuple-element.24.q_ref, bf16[128,128]{1,0:T(8,128)(2,1)S(1)} %get-tuple-element.21.refs_0_, bf16[128,128]{1,0:T(8,128)(2,1)S(1)} %get-tuple-element.22.refs_1_, bf16[256,128]{1,0:T(8,128)(2,1)S(1)} %collective-permute-done.3.refs_2_, ...), custom_call_target="tpu_custom_call" | custom-call | tf_op jit(solution)/shard_map/attend_away/pallas_call | solution.py:174
  18.4 1.0 %collective-permute-start.6 = (bf16[64,64]{1,0:T(8,128)(2,1)S(1)}, bf16[64,64]{1,0:T(8,128)(2,1)S(1)}, u32[]{:S(2)}, u32[]{:S(2)}) collective-permute-start(bf16[64,64]{1,0:T(8,128)(2,1)S(1)} %get-tuple-element.31), channel_id=1, source_target_pairs={{0,3},{1,2},{2,1},{3,0},{4,7},{5,6},{6,5},{7,4},{8,11},{9,10},{10,... | collective-permute-start | bytes 24584 | tf_op jit(solution)/shard_map/ppermute | solution.py:25
  19.4 0.6 %attend_home.1 = (bf16[128,64]{1,0:T(8,128)(2,1)S(1)}, bf16[8,4,8,128]{3,2,1,0:T(8,128)(2,1)}) custom-call(s32[1]{0:T(128)} %bitcast.col_ref, bf16[128,128]{1,0:T(8,128)(2,1)S(1)} %get-tuple-element.20.q_ref, bf16[128,128]{1,0:T(8,128)(2,1)S(1)} %get-tuple-element.21.refs_0_, bf16[128,128]{1,0:T(8,128)(2,1)S(1)} %get-tuple-element.22.refs_1_, ...), custom_call_target="tpu_custom_call" | custom-call | tf_op jit(solution)/shard_map/attend_home/pallas_call | solution.py:206
  20.1 0.7 %collective-permute-start.7 = (bf16[64,64]{1,0:T(8,128)(2,1)S(1)}, bf16[64,64]{1,0:T(8,128)(2,1)S(1)}, u32[]{:S(2)}, u32[]{:S(2)}) collective-permute-start(bf16[64,64]{1,0:T(8,128)(2,1)S(1)} %slice.10), channel_id=1, source_target_pairs={{0,1},{1,0},{2,3},{3,2},{4,5},{5,4},{6,7},{7,6},{8,9},{9,8},{10,11... | collective-permute-start | bytes 24584 | tf_op jit(solution)/shard_map/ppermute | solution.py:25
  20.8 0.5 %collective-permute-start.8 = (bf16[64,64]{1,0:T(8,128)(2,1)S(1)}, bf16[64,64]{1,0:T(8,128)(2,1)S(1)}, u32[]{:S(2)}, u32[]{:S(2)}) collective-permute-start(bf16[64,64]{1,0:T(8,128)(2,1)S(1)} %get-tuple-element.30), channel_id=1, source_target_pairs={{0,2},{1,3},{2,0},{3,1},{4,6},{5,7},{6,4},{7,5},{8,10},{9,11},{10,... | collective-permute-start | bytes 24584 | tf_op jit(solution)/shard_map/ppermute | solution.py:25
  21.3 0.4 %collective-permute-done.6.refs_0_ = bf16[64,64]{1,0:T(8,128)(2,1)S(1)} collective-permute-done((bf16[64,64]{1,0:T(8,128)(2,1)S(1)}, bf16[64,64]{1,0:T(8,128)(2,1)S(1)}, u32[]{:S(2)}, u32[]{:S(2)}) %collective-permute-start.6) | collective-permute-done | bytes 8224 | tf_op jit(solution)/shard_map/ppermute | solution.py:25
  21.7 0.0 collective-permute-done.7.refs_1_
  21.7 0.3 %begin.1.base = f32[64,1280]{1,0:T(8,128)S(1)} custom-call(s32[1]{0:T(128)} %bitcast.col_ref, bf16[128,64]{1,0:T(8,128)(2,1)S(1)} %get-tuple-element.23.home, bf16[64,64]{1,0:T(8,128)(2,1)S(1)} %collective-permute-done.6.refs_0_, bf16[64,64]{1,0:T(8,128)(2,1)S(1)} %collective-permute-done.7.refs_1_, bf16[256,1280]{1,0:T(8,128)(2,1)S(1)} %get-tuple-element.25.refs_2_.w_ref, ...), custom_call_target="tpu_custom_call" | custom-call | tf_op jit(solution)/shard_map/begin/pallas_call | solution.py:241
  22.0 2.5 %collective-permute-done.8.part = bf16[64,64]{1,0:T(8,128)(2,1)S(1)} collective-permute-done((bf16[64,64]{1,0:T(8,128)(2,1)S(1)}, bf16[64,64]{1,0:T(8,128)(2,1)S(1)}, u32[]{:S(2)}, u32[]{:S(2)}) %collective-permute-start.8) | collective-permute-done | bytes 8224 | tf_op jit(solution)/shard_map/ppermute | solution.py:25
  24.5 0.8 %finish.1 = bf16[64,1280]{1,0:T(8,128)(2,1)} custom-call(s32[1]{0:T(128)} %bitcast.col_ref, f32[64,1280]{1,0:T(8,128)S(1)} %begin.1.base, bf16[64,64]{1,0:T(8,128)(2,1)S(1)} %collective-permute-done.8.part, bf16[256,1280]{1,0:T(8,128)(2,1)S(1)} %get-tuple-element.25.refs_2_.w_ref), custom_call_target="tpu_custom_call" | custom-call | tf_op jit(solution)/shard_map/finish/pallas_call | solution.py:269
  (2 shorter events, 0.0 us)
Async XLA Ops:
  0.6 7.4 %collective-permute-start.1 = (bf16[64,1280]{1,0:T(8,128)(2,1)}, bf16[64,1280]{1,0:T(8,128)(2,1)S(1)}, u32[]{:S(2)}, u32[]{:S(2)}) collective-permute-start(bf16[64,1280]{1,0:T(8,128)(2,1)} %bitcast.9), channel_id=1, source_target_pairs={{0,2},{1,3},{2,0},{3,1},{4,6},{5,7},{6,4},{7,5},{8,10},{9,11},{10,... | collective-permute-start | bytes 491528 | tf_op jit(solution)/shard_map/ppermute | solution.py:25
  3.7 11.7 %collective-permute-start = (bf16[64,1280]{1,0:T(8,128)(2,1)}, bf16[64,1280]{1,0:T(8,128)(2,1)S(1)}, u32[]{:S(2)}, u32[]{:S(2)}) collective-permute-start(bf16[64,1280]{1,0:T(8,128)(2,1)} %bitcast.10), channel_id=1, source_target_pairs={{0,1},{1,0},{2,3},{3,2},{4,5},{5,4},{6,7},{7,6},{8,9},{9,8},{10,11... | collective-permute-start | bytes 491528 | tf_op jit(solution)/shard_map/ppermute | solution.py:25
  8.1 7.3 %collective-permute-start.2 = (bf16[64,1280]{1,0:T(8,128)(2,1)S(1)}, bf16[64,1280]{1,0:T(8,128)(2,1)S(1)}, u32[]{:S(2)}, u32[]{:S(2)}) collective-permute-start(bf16[64,1280]{1,0:T(8,128)(2,1)S(1)} %collective-permute-done.1.refs_2_), channel_id=1, source_target_pairs={{0,1},{1,0},{2,3},{3,2},{4,5},{5,4},{6,7},{7,6},{8,9},{9,8},{10,11... | collective-permute-start | bytes 491528 | tf_op jit(solution)/shard_map/ppermute | solution.py:25
  8.1 8.2 %collective-permute-start.3 = (bf16[256,128]{1,0:T(8,128)(2,1)}, bf16[256,128]{1,0:T(8,128)(2,1)S(1)}, u32[]{:S(2)}, u32[]{:S(2)}) collective-permute-start(bf16[256,128]{1,0:T(8,128)(2,1)} %bitcast.13), channel_id=1, source_target_pairs={{0,4},{4,12},{12,8},{8,0},{1,5},{5,13},{13,9},{9,1},{2,6},{6,14},{... | collective-permute-start | bytes 196616 | tf_op jit(solution)/shard_map/ppermute | solution.py:46
  9.9 7.1 %collective-permute-start.4 = (bf16[256,128]{1,0:T(8,128)(2,1)}, bf16[256,128]{1,0:T(8,128)(2,1)S(1)}, u32[]{:S(2)}, u32[]{:S(2)}) collective-permute-start(bf16[256,128]{1,0:T(8,128)(2,1)} %bitcast.14), channel_id=1, source_target_pairs={{0,12},{4,8},{12,0},{8,4},{1,13},{5,9},{13,1},{9,5},{2,14},{6,10},... | collective-permute-start | bytes 196616 | tf_op jit(solution)/shard_map/ppermute | solution.py:46
  12.4 5.4 %collective-permute-start.5 = (bf16[256,128]{1,0:T(8,128)(2,1)}, bf16[256,128]{1,0:T(8,128)(2,1)S(1)}, u32[]{:S(2)}, u32[]{:S(2)}) collective-permute-start(bf16[256,128]{1,0:T(8,128)(2,1)} %bitcast.15), channel_id=1, source_target_pairs={{0,8},{4,0},{12,4},{8,12},{1,9},{5,1},{13,5},{9,13},{2,10},{6,2},{... | collective-permute-start | bytes 196616 | tf_op jit(solution)/shard_map/ppermute | solution.py:46
  18.4 3.4 %collective-permute-start.6 = (bf16[64,64]{1,0:T(8,128)(2,1)S(1)}, bf16[64,64]{1,0:T(8,128)(2,1)S(1)}, u32[]{:S(2)}, u32[]{:S(2)}) collective-permute-start(bf16[64,64]{1,0:T(8,128)(2,1)S(1)} %get-tuple-element.31), channel_id=1, source_target_pairs={{0,3},{1,2},{2,1},{3,0},{4,7},{5,6},{6,5},{7,4},{8,11},{9,10},{10,... | collective-permute-start | bytes 24584 | tf_op jit(solution)/shard_map/ppermute | solution.py:25
  20.1 1.7 %collective-permute-start.7 = (bf16[64,64]{1,0:T(8,128)(2,1)S(1)}, bf16[64,64]{1,0:T(8,128)(2,1)S(1)}, u32[]{:S(2)}, u32[]{:S(2)}) collective-permute-start(bf16[64,64]{1,0:T(8,128)(2,1)S(1)} %slice.10), channel_id=1, source_target_pairs={{0,1},{1,0},{2,3},{3,2},{4,5},{5,4},{6,7},{7,6},{8,9},{9,8},{10,11... | collective-permute-start | bytes 24584 | tf_op jit(solution)/shard_map/ppermute | solution.py:25
  20.8 3.7 %collective-permute-start.8 = (bf16[64,64]{1,0:T(8,128)(2,1)S(1)}, bf16[64,64]{1,0:T(8,128)(2,1)S(1)}, u32[]{:S(2)}, u32[]{:S(2)}) collective-permute-start(bf16[64,64]{1,0:T(8,128)(2,1)S(1)} %get-tuple-element.30), channel_id=1, source_target_pairs={{0,2},{1,3},{2,0},{3,1},{4,6},{5,7},{6,4},{7,5},{8,10},{9,11},{10,... | collective-permute-start | bytes 24584 | tf_op jit(solution)/shard_map/ppermute | solution.py:25

commit v4 on v3

--- a/solution.py
+++ b/solution.py
@@ -142,7 +142,8 @@
             total = part_sum if total is None else total + part_sum
             weighted = part if weighted is None else weighted + part
             start += size
-        out_ref[rows, :] = (weighted[:, head_size:] / total).astype(jnp.bfloat16)
+        skipped = weighted.shape[1] - out_ref.shape[1]
+        out_ref[rows, :] = (weighted[:, skipped:] / total).astype(jnp.bfloat16)
 
     steps = q_ref.shape[0] // tile
     if steps == 1:
@@ -165,18 +166,43 @@
 
 
 def away_kernel(blocks, head_size, tile, q_ref, *refs):
-    attend_rows(head_size, tile, q_ref, refs[:blocks], *refs[blocks:])
-
-
-def attend_away(queries, keys, head_size):
+    *packed, whole, scores = refs[blocks:]
+    attend_rows(head_size, tile, q_ref, refs[:blocks], whole, scores)
+    for index, out_ref in enumerate(packed):
+        rows = out_ref.shape[0]
+        start = 2 * rows * index
+        out_ref[...] = jnp.concatenate(
+            [
+                whole[start : start + rows, head_size:],
+                whole[start + rows : start + 2 * rows, head_size:],
+            ],
+            axis=1,
+        )
+
+
+def product_of(part, weights):
+    head_size = weights.shape[0]
+    if part.shape[1] != head_size:
+        lane = lax.broadcasted_iota(jnp.int32, part.shape, 1)
+        zeros = jnp.zeros_like(part)
+        part = jnp.concatenate(
+            [jnp.where(lane < head_size, part, zeros), jnp.where(lane < head_size, zeros, part)],
+            axis=0,
+        )
+        weights = jnp.concatenate([weights, weights], axis=0)
+    return jnp.dot(part, weights, preferred_element_type=jnp.float32)
+
+
+def attend_away(queries, keys, head_size, each):
     rows = queries.shape[0]
     tile, scores = score_tile(rows, keys)
+    count = rows // each
     return pl.pallas_call(
         functools.partial(away_kernel, len(keys), head_size, tile),
-        out_shape=pltpu.VMEM((rows, head_size), jnp.bfloat16),
+        out_shape=(pltpu.VMEM((each // 2, 2 * head_size), jnp.bfloat16),) * count,
         in_specs=[VMEM] * (1 + len(keys)),
-        out_specs=VMEM,
-        scratch_shapes=[scores],
+        out_specs=(VMEM,) * count,
+        scratch_shapes=[pltpu.VMEM(queries.shape, jnp.bfloat16), scores],
         compiler_params=PARAMS,
         name="attend_away",
     )(*near(queries, *keys))
@@ -231,9 +257,7 @@
     head_size = home.shape[1]
     total = bias[...].reshape(1, -1) + hidden[...].astype(jnp.float32)
     for mask, part in zip((0, *masks), (home[: hidden.shape[0], :], *(p[...] for p in parts))):
-        total = total + jnp.dot(
-            part, head_rows(col_ref, mask, w_ref, head_size), preferred_element_type=jnp.float32
-        )
+        total = total + product_of(part, head_rows(col_ref, mask, w_ref, head_size))
     out_ref[...] = total
 
 
@@ -249,14 +273,15 @@
 
 
 def finish_kernel(mask, col_ref, base, part, w_ref, out_ref, ready, sent):
-    rows = head_rows(col_ref, mask, w_ref, part.shape[1])
+    head_size = part.shape[0] * part.shape[1] // base.shape[0]
+    rows = head_rows(col_ref, mask, w_ref, head_size)
     values = part[...]
     channels = base.shape[1]
     step = channels // 2 if channels % 256 == 0 else channels
     copies = []
     for index, start in enumerate(range(0, channels, step)):
         columns = slice(start, start + step)
-        product = jnp.dot(values, rows[:, columns], preferred_element_type=jnp.float32)
+        product = product_of(values, rows[:, columns])
         ready[:, columns] = (base[:, columns] + product).astype(jnp.bfloat16)
         copy = pltpu.make_async_copy(ready.at[:, columns], out_ref.at[:, columns], sent.at[index])
         copy.start()
@@ -292,14 +317,14 @@
     )
     q_home, kv_home, q_away, kv_away = project([near_own, *strips[1:]], params)
     keys = [kv_home, kv_away] + stale
-    away = attend_away(q_away, keys, head_size)
+    away = attend_away(q_away, keys, head_size, each)
     fresh_shape = (band_rows, size, strip_cols, 2 * head_size)
     home, fresh = attend_home(col, q_home, keys, head_size, fresh_shape)
     mine = {}
     for mask in range(size - 1, 0, -1):
-        block = away if mask >= half else home
         at = (mask % half) * each
-        mine[mask] = swap(block[at : at + each], "cols", mask)
+        block = away[mask - half] if mask >= half else home[at : at + each]
+        mine[mask] = swap(block, "cols", mask)
     last = mine.pop(half)
     base = begin(col, home, mine, near_out, near_bias, near_own)
     output = finish(col, base, half, last, near_out)

time: 25.5 us -> 25.4 us (level)
  no operation moved by 1% of the time
where the time goes in v4:
time: 25.4 us; the launch traced here: 25.2 us
  starting transfers between devices  11.1 us (44%)
  waiting for transfers between devices  8.73 us (34%)
  Pallas kernels  4.64 us (18%)
  between operations  0.71 us (3%)
    ppermute x6, waiting for transfers between devices, swap(): return lax.ppermute(block, axis, [(i, i ^ mask) for i in range(size)])  7.24 us
    ppermute x3, starting transfers between devices, gather_bands(): blocks.append(lax.ppermute(block, axis, pairs))  5.88 us
    ppermute x6, starting transfers between devices, swap(): return lax.ppermute(block, axis, [(i, i ^ mask) for i in range(size)])  5.26 us
    ppermute x3, waiting for transfers between devices, gather_bands(): blocks.append(lax.ppermute(block, axis, pairs))  1.49 us
    pallas_call x1, Pallas kernels, load(): pl.pallas_call(functools.partial(load_kernel, count), out_shape=tuple((pl...  1.41 us
    pallas_call x1, Pallas kernels, finish(): pl.pallas_call(functools.partial(finish_kernel, mask), out_shape=jax.Shap...  0.85 us
    pallas_call x1, Pallas kernels, project(): pl.pallas_call(functools.partial(project_kernel, len(strips)), out_shape=...  0.83 us
    pallas_call x1, Pallas kernels, attend_home(): pl.pallas_call(functools.partial(home_kernel, len(keys), head_size, tile)...  0.65 us
  transfers between devices with their start and end apart: 9, of which 5 were waited for; matrix products, arithmetic and copies ran while one was open for 0% of the time, Pallas kernels for 12%

profile of v4, /device:TPU:0, one launch (start us, length us, event | category | flops | bytes accessed | tf_op | source)
XLA Modules:
  0.0 25.2 jit_solution(4429340045462203539)
XLA Ops:
  0.6 3.0 %collective-permute-start.1 = (bf16[64,1280]{1,0:T(8,128)(2,1)}, bf16[64,1280]{1,0:T(8,128)(2,1)S(1)}, u32[]{:S(2)}, u32[]{:S(2)}) collective-permute-start(bf16[64,1280]{1,0:T(8,128)(2,1)} %bitcast.9), channel_id=1, source_target_pairs={{0,2},{1,3},{2,0},{3,1},{4,6},{5,7},{6,4},{7,5},{8,10},{9,11},{10,... | collective-permute-start | bytes 491528 | tf_op jit(solution)/shard_map/ppermute | solution.py:25
  3.7 0.0 collective-permute-start
  3.7 4.4 %collective-permute-done.1.refs_2_ = bf16[64,1280]{1,0:T(8,128)(2,1)S(1)} collective-permute-done((bf16[64,1280]{1,0:T(8,128)(2,1)}, bf16[64,1280]{1,0:T(8,128)(2,1)S(1)}, u32[]{:S(2)}, u32[]{:S(2)}) %collective-permute-start.1) | collective-permute-done | bytes 163872 | tf_op jit(solution)/shard_map/ppermute | solution.py:25
  8.1 0.0 collective-permute-start.2
  8.1 1.8 %collective-permute-start.3 = (bf16[256,128]{1,0:T(8,128)(2,1)}, bf16[256,128]{1,0:T(8,128)(2,1)S(1)}, u32[]{:S(2)}, u32[]{:S(2)}) collective-permute-start(bf16[256,128]{1,0:T(8,128)(2,1)} %bitcast.13), channel_id=1, source_target_pairs={{0,4},{4,12},{12,8},{8,0},{1,5},{5,13},{13,9},{9,1},{2,6},{6,14},{... | collective-permute-start | bytes 196616 | tf_op jit(solution)/shard_map/ppermute | solution.py:46
  9.9 2.5 %collective-permute-start.4 = (bf16[256,128]{1,0:T(8,128)(2,1)}, bf16[256,128]{1,0:T(8,128)(2,1)S(1)}, u32[]{:S(2)}, u32[]{:S(2)}) collective-permute-start(bf16[256,128]{1,0:T(8,128)(2,1)} %bitcast.14), channel_id=1, source_target_pairs={{0,12},{4,8},{12,0},{8,4},{1,13},{5,9},{13,1},{9,5},{2,14},{6,10},... | collective-permute-start | bytes 196616 | tf_op jit(solution)/shard_map/ppermute | solution.py:46
  12.4 1.6 %collective-permute-start.5 = (bf16[256,128]{1,0:T(8,128)(2,1)}, bf16[256,128]{1,0:T(8,128)(2,1)S(1)}, u32[]{:S(2)}, u32[]{:S(2)}) collective-permute-start(bf16[256,128]{1,0:T(8,128)(2,1)} %bitcast.15), channel_id=1, source_target_pairs={{0,8},{4,0},{12,4},{8,12},{1,9},{5,1},{13,5},{9,13},{2,10},{6,2},{... | collective-permute-start | bytes 196616 | tf_op jit(solution)/shard_map/ppermute | solution.py:46
  14.0 1.4 %load.1 = (bf16[64,1280]{1,0:T(8,128)(2,1)S(1)}, bf16[256,1280]{1,0:T(8,128)(2,1)S(1)}, f32[1280]{0:T(1024)S(1)}, f32[1280]{0:T(1024)S(1)}, f32[1280]{0:T(1024)S...) custom-call(bf16[64,1280]{1,0:T(8,128)(2,1)} %bitcast.11, bf16[256,1280]{1,0:T(8,128)(2,1)} %refs_1_.1, ...), custom_call_target="tpu_custom_call" | custom-call | tf_op jit(solution)/shard_map/load/pallas_call | solution.py:72
  15.4 0.0 collective-permute-done.refs_1_
  15.4 0.0 collective-permute-done.2.refs_3_
  15.4 0.8 %project.1 = (bf16[128,128]{1,0:T(8,128)(2,1)S(1)}, bf16[128,128]{1,0:T(8,128)(2,1)S(1)}, bf16[128,128]{1,0:T(8,128)(2,1)S(1)}, bf16[128,128]{1,0:T(8,128)(2,1)S(1)}) custom-call(bf16[64,1280]{1,0:T(8,128)(2,1)S(1)} %get-tuple-element.17.refs_0_.refs_4_, bf16[64,1280]{1,0:T(8,128)(2,1)S(1)} %collective-permute-done.refs_1_, ...), custom_call_target="tpu_custom_call" | custom-call | tf_op jit(solution)/shard_map/project/pallas_call | solution.py:109
  16.2 0.0 collective-permute-done.3.refs_2_
  16.2 0.7 %collective-permute-done.4.refs_3_ = bf16[256,128]{1,0:T(8,128)(2,1)S(1)} collective-permute-done((bf16[256,128]{1,0:T(8,128)(2,1)}, bf16[256,128]{1,0:T(8,128)(2,1)S(1)}, u32[]{:S(2)}, u32[]{:S(2)}) %collective-permute-start.4) | collective-permute-done | bytes 65568 | tf_op jit(solution)/shard_map/ppermute | solution.py:46
  17.0 0.8 %collective-permute-done.5.refs_4_ = bf16[256,128]{1,0:T(8,128)(2,1)S(1)} collective-permute-done((bf16[256,128]{1,0:T(8,128)(2,1)}, bf16[256,128]{1,0:T(8,128)(2,1)S(1)}, u32[]{:S(2)}, u32[]{:S(2)}) %collective-permute-start.5) | collective-permute-done | bytes 65568 | tf_op jit(solution)/shard_map/ppermute | solution.py:46
  17.7 0.6 %attend_home.1 = (bf16[128,64]{1,0:T(8,128)(2,1)S(1)}, bf16[8,4,8,128]{3,2,1,0:T(8,128)(2,1)}) custom-call(s32[1]{0:T(128)} %bitcast.col_ref, bf16[128,128]{1,0:T(8,128)(2,1)S(1)} %get-tuple-element.22.q_ref, bf16[128,128]{1,0:T(8,128)(2,1)S(1)} %get-tuple-element.23.refs_0_, bf16[128,128]{1,0:T(8,128)(2,1)S(1)} %get-tuple-element.24.refs_1_, ...), custom_call_target="tpu_custom_call" | custom-call | tf_op jit(solution)/shard_map/attend_home/pallas_call | solution.py:232
  18.4 0.1 collective-permute-start.7
  18.5 0.6 %attend_away.1 = (bf16[32,128]{1,0:T(8,128)(2,1)S(1)}, bf16[32,128]{1,0:T(8,128)(2,1)S(1)}) custom-call(bf16[128,128]{1,0:T(8,128)(2,1)S(1)} %get-tuple-element.26.q_ref, bf16[128,128]{1,0:T(8,128)(2,1)S(1)} %get-tuple-element.23.refs_0_, bf16[128,128]{1,0:T(8,128)(2,1)S(1)} %get-tuple-element.24.refs_1_, ...), custom_call_target="tpu_custom_call" | custom-call | tf_op jit(solution)/shard_map/attend_away/pallas_call | solution.py:200
  19.1 1.6 %collective-permute-start.6 = (bf16[32,128]{1,0:T(8,128)(2,1)S(1)}, bf16[32,128]{1,0:T(8,128)(2,1)S(1)}, u32[]{:S(2)}, u32[]{:S(2)}) collective-permute-start(bf16[32,128]{1,0:T(8,128)(2,1)S(1)} %get-tuple-element.27), channel_id=1, source_target_pairs={{0,3},{1,2},{2,1},{3,0},{4,7},{5,6},{6,5},{7,4},{8,11},{9,10},{10,... | collective-permute-start | bytes 24584 | tf_op jit(solution)/shard_map/ppermute | solution.py:25
  20.7 0.5 %collective-permute-start.8 = (bf16[32,128]{1,0:T(8,128)(2,1)S(1)}, bf16[32,128]{1,0:T(8,128)(2,1)S(1)}, u32[]{:S(2)}, u32[]{:S(2)}) collective-permute-start(bf16[32,128]{1,0:T(8,128)(2,1)S(1)} %get-tuple-element.30), channel_id=1, source_target_pairs={{0,2},{1,3},{2,0},{3,1},{4,6},{5,7},{6,4},{7,5},{8,10},{9,11},{10,... | collective-permute-start | bytes 24584 | tf_op jit(solution)/shard_map/ppermute | solution.py:25
  21.3 0.0 collective-permute-done.7.refs_1_
  21.3 1.0 %collective-permute-done.6.refs_0_ = bf16[32,128]{1,0:T(8,128)(2,1)S(1)} collective-permute-done((bf16[32,128]{1,0:T(8,128)(2,1)S(1)}, bf16[32,128]{1,0:T(8,128)(2,1)S(1)}, u32[]{:S(2)}, u32[]{:S(2)}) %collective-permute-start.6) | collective-permute-done | bytes 8224 | tf_op jit(solution)/shard_map/ppermute | solution.py:25
  22.2 0.3 %begin.1.base = f32[64,1280]{1,0:T(8,128)S(1)} custom-call(s32[1]{0:T(128)} %bitcast.col_ref, bf16[128,64]{1,0:T(8,128)(2,1)S(1)} %get-tuple-element.25.home, bf16[32,128]{1,0:T(8,128)(2,1)S(1)} %collective-permute-done.6.refs_0_, bf16[64,64]{1,0:T(8,128)(2,1)S(1)} %collective-permute-done.7.refs_1_, bf16[256,1280]{1,0:T(8,128)(2,1)S(1)} %get-tuple-element.28.refs_2_.w_ref, ...), custom_call_target="tpu_custom_call" | custom-call | tf_op jit(solution)/shard_map/begin/pallas_call | solution.py:265
  22.5 1.9 %collective-permute-done.8.part = bf16[32,128]{1,0:T(8,128)(2,1)S(1)} collective-permute-done((bf16[32,128]{1,0:T(8,128)(2,1)S(1)}, bf16[32,128]{1,0:T(8,128)(2,1)S(1)}, u32[]{:S(2)}, u32[]{:S(2)}) %collective-permute-start.8) | collective-permute-done | bytes 8224 | tf_op jit(solution)/shard_map/ppermute | solution.py:25
  24.4 0.9 %finish.1 = bf16[64,1280]{1,0:T(8,128)(2,1)} custom-call(s32[1]{0:T(128)} %bitcast.col_ref, f32[64,1280]{1,0:T(8,128)S(1)} %begin.1.base, bf16[32,128]{1,0:T(8,128)(2,1)S(1)} %collective-permute-done.8.part, bf16[256,1280]{1,0:T(8,128)(2,1)S(1)} %get-tuple-element.28.refs_2_.w_ref), custom_call_target="tpu_custom_call" | custom-call | tf_op jit(solution)/shard_map/finish/pallas_call | solution.py:294
  (1 shorter events, 0.0 us)
Async XLA Ops:
  0.6 7.4 %collective-permute-start.1 = (bf16[64,1280]{1,0:T(8,128)(2,1)}, bf16[64,1280]{1,0:T(8,128)(2,1)S(1)}, u32[]{:S(2)}, u32[]{:S(2)}) collective-permute-start(bf16[64,1280]{1,0:T(8,128)(2,1)} %bitcast.9), channel_id=1, source_target_pairs={{0,2},{1,3},{2,0},{3,1},{4,6},{5,7},{6,4},{7,5},{8,10},{9,11},{10,... | collective-permute-start | bytes 491528 | tf_op jit(solution)/shard_map/ppermute | solution.py:25
  3.7 11.7 %collective-permute-start = (bf16[64,1280]{1,0:T(8,128)(2,1)}, bf16[64,1280]{1,0:T(8,128)(2,1)S(1)}, u32[]{:S(2)}, u32[]{:S(2)}) collective-permute-start(bf16[64,1280]{1,0:T(8,128)(2,1)} %bitcast.10), channel_id=1, source_target_pairs={{0,1},{1,0},{2,3},{3,2},{4,5},{5,4},{6,7},{7,6},{8,9},{9,8},{10,11... | collective-permute-start | bytes 491528 | tf_op jit(solution)/shard_map/ppermute | solution.py:25
  8.1 7.3 %collective-permute-start.2 = (bf16[64,1280]{1,0:T(8,128)(2,1)S(1)}, bf16[64,1280]{1,0:T(8,128)(2,1)S(1)}, u32[]{:S(2)}, u32[]{:S(2)}) collective-permute-start(bf16[64,1280]{1,0:T(8,128)(2,1)S(1)} %collective-permute-done.1.refs_2_), channel_id=1, source_target_pairs={{0,1},{1,0},{2,3},{3,2},{4,5},{5,4},{6,7},{7,6},{8,9},{9,8},{10,11... | collective-permute-start | bytes 491528 | tf_op jit(solution)/shard_map/ppermute | solution.py:25
  8.1 8.2 %collective-permute-start.3 = (bf16[256,128]{1,0:T(8,128)(2,1)}, bf16[256,128]{1,0:T(8,128)(2,1)S(1)}, u32[]{:S(2)}, u32[]{:S(2)}) collective-permute-start(bf16[256,128]{1,0:T(8,128)(2,1)} %bitcast.13), channel_id=1, source_target_pairs={{0,4},{4,12},{12,8},{8,0},{1,5},{5,13},{13,9},{9,1},{2,6},{6,14},{... | collective-permute-start | bytes 196616 | tf_op jit(solution)/shard_map/ppermute | solution.py:46
  9.9 7.1 %collective-permute-start.4 = (bf16[256,128]{1,0:T(8,128)(2,1)}, bf16[256,128]{1,0:T(8,128)(2,1)S(1)}, u32[]{:S(2)}, u32[]{:S(2)}) collective-permute-start(bf16[256,128]{1,0:T(8,128)(2,1)} %bitcast.14), channel_id=1, source_target_pairs={{0,12},{4,8},{12,0},{8,4},{1,13},{5,9},{13,1},{9,5},{2,14},{6,10},... | collective-permute-start | bytes 196616 | tf_op jit(solution)/shard_map/ppermute | solution.py:46
  12.4 5.4 %collective-permute-start.5 = (bf16[256,128]{1,0:T(8,128)(2,1)}, bf16[256,128]{1,0:T(8,128)(2,1)S(1)}, u32[]{:S(2)}, u32[]{:S(2)}) collective-permute-start(bf16[256,128]{1,0:T(8,128)(2,1)} %bitcast.15), channel_id=1, source_target_pairs={{0,8},{4,0},{12,4},{8,12},{1,9},{5,1},{13,5},{9,13},{2,10},{6,2},{... | collective-permute-start | bytes 196616 | tf_op jit(solution)/shard_map/ppermute | solution.py:46
  18.4 2.9 %collective-permute-start.7 = (bf16[64,64]{1,0:T(8,128)(2,1)S(1)}, bf16[64,64]{1,0:T(8,128)(2,1)S(1)}, u32[]{:S(2)}, u32[]{:S(2)}) collective-permute-start(bf16[64,64]{1,0:T(8,128)(2,1)S(1)} %slice.3), channel_id=1, source_target_pairs={{0,1},{1,0},{2,3},{3,2},{4,5},{5,4},{6,7},{7,6},{8,9},{9,8},{10,11... | collective-permute-start | bytes 24584 | tf_op jit(solution)/shard_map/ppermute | solution.py:25
  19.1 3.1 %collective-permute-start.6 = (bf16[32,128]{1,0:T(8,128)(2,1)S(1)}, bf16[32,128]{1,0:T(8,128)(2,1)S(1)}, u32[]{:S(2)}, u32[]{:S(2)}) collective-permute-start(bf16[32,128]{1,0:T(8,128)(2,1)S(1)} %get-tuple-element.27), channel_id=1, source_target_pairs={{0,3},{1,2},{2,1},{3,0},{4,7},{5,6},{6,5},{7,4},{8,11},{9,10},{10,... | collective-permute-start | bytes 24584 | tf_op jit(solution)/shard_map/ppermute | solution.py:25
  20.7 3.7 %collective-permute-start.8 = (bf16[32,128]{1,0:T(8,128)(2,1)S(1)}, bf16[32,128]{1,0:T(8,128)(2,1)S(1)}, u32[]{:S(2)}, u32[]{:S(2)}) collective-permute-start(bf16[32,128]{1,0:T(8,128)(2,1)S(1)} %get-tuple-element.30), channel_id=1, source_target_pairs={{0,2},{1,3},{2,0},{3,1},{4,6},{5,7},{6,4},{7,5},{8,10},{9,11},{10,... | collective-permute-start | bytes 24584 | tf_op jit(solution)/shard_map/ppermute | solution.py:25

commit v5 on v4

--- a/solution.py
+++ b/solution.py
@@ -168,6 +168,10 @@
 def away_kernel(blocks, head_size, tile, q_ref, *refs):
     *packed, whole, scores = refs[blocks:]
     attend_rows(head_size, tile, q_ref, refs[:blocks], whole, scores)
+    pack(whole, packed, head_size)
+
+
+def pack(whole, packed, head_size):
     for index, out_ref in enumerate(packed):
         rows = out_ref.shape[0]
         start = 2 * rows * index
@@ -209,7 +213,7 @@
 
 
 def home_kernel(blocks, head_size, tile, col_ref, q_ref, *refs):
-    keys, (out_ref, fresh_out, scores, fresh, sent) = refs[:blocks], refs[blocks:]
+    keys, (*packed, fresh_out, whole, scores, fresh, sent) = refs[:blocks], refs[blocks:]
     rows, count, width, lanes = fresh.shape
     each = rows * width
     for mask in range(count):
@@ -221,7 +225,8 @@
 
     @pl.when(col_ref[0] >= 0)
     def _():
-        attend_rows(head_size, tile, q_ref, keys, out_ref, scores)
+        attend_rows(head_size, tile, q_ref, keys, whole, scores)
+        pack(whole, packed, head_size)
 
     copy.wait()
 
@@ -229,15 +234,18 @@
 def attend_home(col, queries, keys, head_size, fresh_shape):
     rows = queries.shape[0]
     tile, scores = score_tile(rows, keys)
+    each = fresh_shape[0] * fresh_shape[2]
+    count = rows // each
     return pl.pallas_call(
         functools.partial(home_kernel, len(keys), head_size, tile),
         out_shape=(
-            pltpu.VMEM((rows, head_size), jnp.bfloat16),
+            *((pltpu.VMEM((each // 2, 2 * head_size), jnp.bfloat16),) * count),
             jax.ShapeDtypeStruct(fresh_shape, jnp.bfloat16),
         ),
         in_specs=[SMEM] + [VMEM] * (1 + len(keys)),
-        out_specs=(VMEM, HBM),
+        out_specs=(VMEM,) * count + (HBM,),
         scratch_shapes=[
+            pltpu.VMEM(queries.shape, jnp.bfloat16),
             scores,
             pltpu.VMEM(fresh_shape, jnp.bfloat16),
             pltpu.SemaphoreType.DMA,
@@ -254,9 +262,9 @@
 
 def begin_kernel(masks, col_ref, home, *refs):
     *parts, w_ref, bias, hidden, out_ref = refs
-    head_size = home.shape[1]
+    head_size = home.shape[0] * home.shape[1] // hidden.shape[0]
     total = bias[...].reshape(1, -1) + hidden[...].astype(jnp.float32)
-    for mask, part in zip((0, *masks), (home[: hidden.shape[0], :], *(p[...] for p in parts))):
+    for mask, part in zip((0, *masks), (home[...], *(p[...] for p in parts))):
         total = total + product_of(part, head_rows(col_ref, mask, w_ref, head_size))
     out_ref[...] = total
 
@@ -319,14 +327,13 @@
     keys = [kv_home, kv_away] + stale
     away = attend_away(q_away, keys, head_size, each)
     fresh_shape = (band_rows, size, strip_cols, 2 * head_size)
-    home, fresh = attend_home(col, q_home, keys, head_size, fresh_shape)
+    *home, fresh = attend_home(col, q_home, keys, head_size, fresh_shape)
     mine = {}
     for mask in range(size - 1, 0, -1):
-        at = (mask % half) * each
-        block = away[mask - half] if mask >= half else home[at : at + each]
+        block = away[mask - half] if mask >= half else home[mask]
         mine[mask] = swap(block, "cols", mask)
     last = mine.pop(half)
-    base = begin(col, home, mine, near_out, near_bias, near_own)
+    base = begin(col, home[0], mine, near_out, near_bias, near_own)
     output = finish(col, base, half, last, near_out)
     return (
         output.reshape(hidden.shape),

time: 25.4 us -> 25.4 us (level)
  transfers between devices with their start and end apart: 9 -> 9, of which waited for: 5 -> 5; matrix products, arithmetic and copies ran while one was open for 0% -> 0% of each run, Pallas kernels for 12% -> 13%
where the time goes in v5:
time: 25.4 us; the launch traced here: 25.2 us
  starting transfers between devices  11.2 us (44%)
  waiting for transfers between devices  8.72 us (34%)
  Pallas kernels  4.66 us (18%)
  between operations  0.69 us (3%)
    ppermute x6, waiting for transfers between devices, swap(): return lax.ppermute(block, axis, [(i, i ^ mask) for i in range(size)])  7.22 us
    ppermute x3, starting transfers between devices, gather_bands(): blocks.append(lax.ppermute(block, axis, pairs))  5.88 us
    ppermute x6, starting transfers between devices, swap(): return lax.ppermute(block, axis, [(i, i ^ mask) for i in range(size)])  5.27 us
    ppermute x3, waiting for transfers between devices, gather_bands(): blocks.append(lax.ppermute(block, axis, pairs))  1.49 us
    pallas_call x1, Pallas kernels, load(): pl.pallas_call(functools.partial(load_kernel, count), out_shape=tuple((pl...  1.41 us
    pallas_call x1, Pallas kernels, finish(): pl.pallas_call(functools.partial(finish_kernel, mask), out_shape=jax.Shap...  0.85 us
    pallas_call x1, Pallas kernels, project(): pl.pallas_call(functools.partial(project_kernel, len(strips)), out_shape=...  0.83 us
    pallas_call x1, Pallas kernels, attend_home(): pl.pallas_call(functools.partial(home_kernel, len(keys), head_size, tile)...  0.65 us
  transfers between devices with their start and end apart: 9, of which 5 were waited for; matrix products, arithmetic and copies ran while one was open for 0% of the time, Pallas kernels for 13%

profile of v5, /device:TPU:0, one launch (start us, length us, event | category | flops | bytes accessed | tf_op | source)
XLA Modules:
  0.0 25.2 jit_solution(5027875532320560063)
XLA Ops:
  0.6 3.0 %collective-permute-start.1 = (bf16[64,1280]{1,0:T(8,128)(2,1)}, bf16[64,1280]{1,0:T(8,128)(2,1)S(1)}, u32[]{:S(2)}, u32[]{:S(2)}) collective-permute-start(bf16[64,1280]{1,0:T(8,128)(2,1)} %bitcast.9), channel_id=1, source_target_pairs={{0,2},{1,3},{2,0},{3,1},{4,6},{5,7},{6,4},{7,5},{8,10},{9,11},{10,... | collective-permute-start | bytes 491528 | tf_op jit(solution)/shard_map/ppermute | solution.py:25
  3.7 0.0 collective-permute-start
  3.7 4.4 %collective-permute-done.1.refs_2_ = bf16[64,1280]{1,0:T(8,128)(2,1)S(1)} collective-permute-done((bf16[64,1280]{1,0:T(8,128)(2,1)}, bf16[64,1280]{1,0:T(8,128)(2,1)S(1)}, u32[]{:S(2)}, u32[]{:S(2)}) %collective-permute-start.1) | collective-permute-done | bytes 163872 | tf_op jit(solution)/shard_map/ppermute | solution.py:25
  8.1 0.0 collective-permute-start.2
  8.1 1.8 %collective-permute-start.3 = (bf16[256,128]{1,0:T(8,128)(2,1)}, bf16[256,128]{1,0:T(8,128)(2,1)S(1)}, u32[]{:S(2)}, u32[]{:S(2)}) collective-permute-start(bf16[256,128]{1,0:T(8,128)(2,1)} %bitcast.13), channel_id=1, source_target_pairs={{0,4},{4,12},{12,8},{8,0},{1,5},{5,13},{13,9},{9,1},{2,6},{6,14},{... | collective-permute-start | bytes 196616 | tf_op jit(solution)/shard_map/ppermute | solution.py:46
  9.9 2.5 %collective-permute-start.4 = (bf16[256,128]{1,0:T(8,128)(2,1)}, bf16[256,128]{1,0:T(8,128)(2,1)S(1)}, u32[]{:S(2)}, u32[]{:S(2)}) collective-permute-start(bf16[256,128]{1,0:T(8,128)(2,1)} %bitcast.14), channel_id=1, source_target_pairs={{0,12},{4,8},{12,0},{8,4},{1,13},{5,9},{13,1},{9,5},{2,14},{6,10},... | collective-permute-start | bytes 196616 | tf_op jit(solution)/shard_map/ppermute | solution.py:46
  12.4 1.6 %collective-permute-start.5 = (bf16[256,128]{1,0:T(8,128)(2,1)}, bf16[256,128]{1,0:T(8,128)(2,1)S(1)}, u32[]{:S(2)}, u32[]{:S(2)}) collective-permute-start(bf16[256,128]{1,0:T(8,128)(2,1)} %bitcast.15), channel_id=1, source_target_pairs={{0,8},{4,0},{12,4},{8,12},{1,9},{5,1},{13,5},{9,13},{2,10},{6,2},{... | collective-permute-start | bytes 196616 | tf_op jit(solution)/shard_map/ppermute | solution.py:46
  14.0 1.4 %load.1 = (bf16[64,1280]{1,0:T(8,128)(2,1)S(1)}, bf16[256,1280]{1,0:T(8,128)(2,1)S(1)}, f32[1280]{0:T(1024)S(1)}, f32[1280]{0:T(1024)S(1)}, f32[1280]{0:T(1024)S...) custom-call(bf16[64,1280]{1,0:T(8,128)(2,1)} %bitcast.11, bf16[256,1280]{1,0:T(8,128)(2,1)} %refs_1_.1, ...), custom_call_target="tpu_custom_call" | custom-call | tf_op jit(solution)/shard_map/load/pallas_call | solution.py:72
  15.4 0.0 collective-permute-done.refs_1_
  15.4 0.0 collective-permute-done.2.refs_3_
  15.4 0.8 %project.1 = (bf16[128,128]{1,0:T(8,128)(2,1)S(1)}, bf16[128,128]{1,0:T(8,128)(2,1)S(1)}, bf16[128,128]{1,0:T(8,128)(2,1)S(1)}, bf16[128,128]{1,0:T(8,128)(2,1)S(1)}) custom-call(bf16[64,1280]{1,0:T(8,128)(2,1)S(1)} %get-tuple-element.18.refs_0_.refs_4_, bf16[64,1280]{1,0:T(8,128)(2,1)S(1)} %collective-permute-done.refs_1_, ...), custom_call_target="tpu_custom_call" | custom-call | tf_op jit(solution)/shard_map/project/pallas_call | solution.py:109
  16.2 0.0 collective-permute-done.3.refs_2_
  16.2 0.7 %collective-permute-done.4.refs_3_ = bf16[256,128]{1,0:T(8,128)(2,1)S(1)} collective-permute-done((bf16[256,128]{1,0:T(8,128)(2,1)}, bf16[256,128]{1,0:T(8,128)(2,1)S(1)}, u32[]{:S(2)}, u32[]{:S(2)}) %collective-permute-start.4) | collective-permute-done | bytes 65568 | tf_op jit(solution)/shard_map/ppermute | solution.py:46
  17.0 0.8 %collective-permute-done.5.refs_4_ = bf16[256,128]{1,0:T(8,128)(2,1)S(1)} collective-permute-done((bf16[256,128]{1,0:T(8,128)(2,1)}, bf16[256,128]{1,0:T(8,128)(2,1)S(1)}, u32[]{:S(2)}, u32[]{:S(2)}) %collective-permute-start.5) | collective-permute-done | bytes 65568 | tf_op jit(solution)/shard_map/ppermute | solution.py:46
  17.7 0.6 %attend_away.1 = (bf16[32,128]{1,0:T(8,128)(2,1)S(1)}, bf16[32,128]{1,0:T(8,128)(2,1)S(1)}) custom-call(bf16[128,128]{1,0:T(8,128)(2,1)S(1)} %get-tuple-element.27.q_ref, bf16[128,128]{1,0:T(8,128)(2,1)S(1)} %get-tuple-element.24.refs_0_, bf16[128,128]{1,0:T(8,128)(2,1)S(1)} %get-tuple-element.25.refs_1_, ...), custom_call_target="tpu_custom_call" | custom-call | tf_op jit(solution)/shard_map/attend_away/pallas_call | solution.py:204
  18.4 1.0 %collective-permute-start.6 = (bf16[32,128]{1,0:T(8,128)(2,1)S(1)}, bf16[32,128]{1,0:T(8,128)(2,1)S(1)}, u32[]{:S(2)}, u32[]{:S(2)}) collective-permute-start(bf16[32,128]{1,0:T(8,128)(2,1)S(1)} %get-tuple-element.28), channel_id=1, source_target_pairs={{0,3},{1,2},{2,1},{3,0},{4,7},{5,6},{6,5},{7,4},{8,11},{9,10},{10,... | collective-permute-start | bytes 24584 | tf_op jit(solution)/shard_map/ppermute | solution.py:25
  19.4 0.6 %attend_home.1 = (bf16[32,128]{1,0:T(8,128)(2,1)S(1)}, bf16[32,128]{1,0:T(8,128)(2,1)S(1)}, bf16[8,4,8,128]{3,2,1,0:T(8,128)(2,1)}) custom-call(s32[1]{0:T(128)} %bitcast.col_ref, bf16[128,128]{1,0:T(8,128)(2,1)S(1)} %get-tuple-element.23.q_ref, bf16[128,128]{1,0:T(8,128)(2,1)S(1)} %get-tuple-element.24.refs_0_, ...), custom_call_target="tpu_custom_call" | custom-call | tf_op jit(solution)/shard_map/attend_home/pallas_call | solution.py:239
  20.0 0.7 %collective-permute-start.7 = (bf16[32,128]{1,0:T(8,128)(2,1)S(1)}, bf16[32,128]{1,0:T(8,128)(2,1)S(1)}, u32[]{:S(2)}, u32[]{:S(2)}) collective-permute-start(bf16[32,128]{1,0:T(8,128)(2,1)S(1)} %get-tuple-element.29), channel_id=1, source_target_pairs={{0,1},{1,0},{2,3},{3,2},{4,5},{5,4},{6,7},{7,6},{8,9},{9,8},{10,11... | collective-permute-start | bytes 24584 | tf_op jit(solution)/shard_map/ppermute | solution.py:25
  20.7 0.5 %collective-permute-start.8 = (bf16[32,128]{1,0:T(8,128)(2,1)S(1)}, bf16[32,128]{1,0:T(8,128)(2,1)S(1)}, u32[]{:S(2)}, u32[]{:S(2)}) collective-permute-start(bf16[32,128]{1,0:T(8,128)(2,1)S(1)} %get-tuple-element.32), channel_id=1, source_target_pairs={{0,2},{1,3},{2,0},{3,1},{4,6},{5,7},{6,4},{7,5},{8,10},{9,11},{10,... | collective-permute-start | bytes 24584 | tf_op jit(solution)/shard_map/ppermute | solution.py:25
  21.3 0.2 collective-permute-done.6.refs_0_
  21.5 0.0 collective-permute-done.7.refs_1_
  21.5 0.3 %begin.1.base = f32[64,1280]{1,0:T(8,128)S(1)} custom-call(s32[1]{0:T(128)} %bitcast.col_ref, bf16[32,128]{1,0:T(8,128)(2,1)S(1)} %get-tuple-element.26.home, bf16[32,128]{1,0:T(8,128)(2,1)S(1)} %collective-permute-done.6.refs_0_, bf16[32,128]{1,0:T(8,128)(2,1)S(1)} %collective-permute-done.7.refs_1_, bf16[256,1280]{1,0:T(8,128)(2,1)S(1)} %get-tuple-element.30.refs_2_.w_ref, ...), custom_call_target="tpu_custom_call" | custom-call | tf_op jit(solution)/shard_map/begin/pallas_call | solution.py:273
  21.8 2.5 %collective-permute-done.8.part = bf16[32,128]{1,0:T(8,128)(2,1)S(1)} collective-permute-done((bf16[32,128]{1,0:T(8,128)(2,1)S(1)}, bf16[32,128]{1,0:T(8,128)(2,1)S(1)}, u32[]{:S(2)}, u32[]{:S(2)}) %collective-permute-start.8) | collective-permute-done | bytes 8224 | tf_op jit(solution)/shard_map/ppermute | solution.py:25
  24.4 0.9 %finish.1 = bf16[64,1280]{1,0:T(8,128)(2,1)} custom-call(s32[1]{0:T(128)} %bitcast.col_ref, f32[64,1280]{1,0:T(8,128)S(1)} %begin.1.base, bf16[32,128]{1,0:T(8,128)(2,1)S(1)} %collective-permute-done.8.part, bf16[256,1280]{1,0:T(8,128)(2,1)S(1)} %get-tuple-element.30.refs_2_.w_ref), custom_call_target="tpu_custom_call" | custom-call | tf_op jit(solution)/shard_map/finish/pallas_call | solution.py:302
Async XLA Ops:
  0.6 7.4 %collective-permute-start.1 = (bf16[64,1280]{1,0:T(8,128)(2,1)}, bf16[64,1280]{1,0:T(8,128)(2,1)S(1)}, u32[]{:S(2)}, u32[]{:S(2)}) collective-permute-start(bf16[64,1280]{1,0:T(8,128)(2,1)} %bitcast.9), channel_id=1, source_target_pairs={{0,2},{1,3},{2,0},{3,1},{4,6},{5,7},{6,4},{7,5},{8,10},{9,11},{10,... | collective-permute-start | bytes 491528 | tf_op jit(solution)/shard_map/ppermute | solution.py:25
  3.7 11.7 %collective-permute-start = (bf16[64,1280]{1,0:T(8,128)(2,1)}, bf16[64,1280]{1,0:T(8,128)(2,1)S(1)}, u32[]{:S(2)}, u32[]{:S(2)}) collective-permute-start(bf16[64,1280]{1,0:T(8,128)(2,1)} %bitcast.10), channel_id=1, source_target_pairs={{0,1},{1,0},{2,3},{3,2},{4,5},{5,4},{6,7},{7,6},{8,9},{9,8},{10,11... | collective-permute-start | bytes 491528 | tf_op jit(solution)/shard_map/ppermute | solution.py:25
  8.1 7.3 %collective-permute-start.2 = (bf16[64,1280]{1,0:T(8,128)(2,1)S(1)}, bf16[64,1280]{1,0:T(8,128)(2,1)S(1)}, u32[]{:S(2)}, u32[]{:S(2)}) collective-permute-start(bf16[64,1280]{1,0:T(8,128)(2,1)S(1)} %collective-permute-done.1.refs_2_), channel_id=1, source_target_pairs={{0,1},{1,0},{2,3},{3,2},{4,5},{5,4},{6,7},{7,6},{8,9},{9,8},{10,11... | collective-permute-start | bytes 491528 | tf_op jit(solution)/shard_map/ppermute | solution.py:25
  8.1 8.2 %collective-permute-start.3 = (bf16[256,128]{1,0:T(8,128)(2,1)}, bf16[256,128]{1,0:T(8,128)(2,1)S(1)}, u32[]{:S(2)}, u32[]{:S(2)}) collective-permute-start(bf16[256,128]{1,0:T(8,128)(2,1)} %bitcast.13), channel_id=1, source_target_pairs={{0,4},{4,12},{12,8},{8,0},{1,5},{5,13},{13,9},{9,1},{2,6},{6,14},{... | collective-permute-start | bytes 196616 | tf_op jit(solution)/shard_map/ppermute | solution.py:46
  9.9 7.1 %collective-permute-start.4 = (bf16[256,128]{1,0:T(8,128)(2,1)}, bf16[256,128]{1,0:T(8,128)(2,1)S(1)}, u32[]{:S(2)}, u32[]{:S(2)}) collective-permute-start(bf16[256,128]{1,0:T(8,128)(2,1)} %bitcast.14), channel_id=1, source_target_pairs={{0,12},{4,8},{12,0},{8,4},{1,13},{5,9},{13,1},{9,5},{2,14},{6,10},... | collective-permute-start | bytes 196616 | tf_op jit(solution)/shard_map/ppermute | solution.py:46
  12.4 5.4 %collective-permute-start.5 = (bf16[256,128]{1,0:T(8,128)(2,1)}, bf16[256,128]{1,0:T(8,128)(2,1)S(1)}, u32[]{:S(2)}, u32[]{:S(2)}) collective-permute-start(bf16[256,128]{1,0:T(8,128)(2,1)} %bitcast.15), channel_id=1, source_target_pairs={{0,8},{4,0},{12,4},{8,12},{1,9},{5,1},{13,5},{9,13},{2,10},{6,2},{... | collective-permute-start | bytes 196616 | tf_op jit(solution)/shard_map/ppermute | solution.py:46
  18.4 3.1 %collective-permute-start.6 = (bf16[32,128]{1,0:T(8,128)(2,1)S(1)}, bf16[32,128]{1,0:T(8,128)(2,1)S(1)}, u32[]{:S(2)}, u32[]{:S(2)}) collective-permute-start(bf16[32,128]{1,0:T(8,128)(2,1)S(1)} %get-tuple-element.28), channel_id=1, source_target_pairs={{0,3},{1,2},{2,1},{3,0},{4,7},{5,6},{6,5},{7,4},{8,11},{9,10},{10,... | collective-permute-start | bytes 24584 | tf_op jit(solution)/shard_map/ppermute | solution.py:25
  20.0 1.5 %collective-permute-start.7 = (bf16[32,128]{1,0:T(8,128)(2,1)S(1)}, bf16[32,128]{1,0:T(8,128)(2,1)S(1)}, u32[]{:S(2)}, u32[]{:S(2)}) collective-permute-start(bf16[32,128]{1,0:T(8,128)(2,1)S(1)} %get-tuple-element.29), channel_id=1, source_target_pairs={{0,1},{1,0},{2,3},{3,2},{4,5},{5,4},{6,7},{7,6},{8,9},{9,8},{10,11... | collective-permute-start | bytes 24584 | tf_op jit(solution)/shard_map/ppermute | solution.py:25
  20.7 3.7 %collective-permute-start.8 = (bf16[32,128]{1,0:T(8,128)(2,1)S(1)}, bf16[32,128]{1,0:T(8,128)(2,1)S(1)}, u32[]{:S(2)}, u32[]{:S(2)}) collective-permute-start(bf16[32,128]{1,0:T(8,128)(2,1)S(1)} %get-tuple-element.32), channel_id=1, source_target_pairs={{0,2},{1,3},{2,0},{3,1},{4,6},{5,7},{6,4},{7,5},{8,10},{9,11},{10,... | collective-permute-start | bytes 24584 | tf_op jit(solution)/shard_map/ppermute | solution.py:25
